TPU v7x, 512 devices: a whole 4x8x8 slice. The times are simulated.
512 devices in a mesh: src: 32 (over y_hi, x, core), tgt: 16 (over z, y_lo).
Axes of the slice: x: 4, y: 8 (y_hi: 4, y_lo: 2; y = y_hi * 2 + y_lo), z: 8, core: 2. Of those that a mesh axis runs over, the one named last changes fastest.
Arguments:
- feat_in: bfloat16 [512, 49, 128], P(('src', 'tgt')), may hold values from -6 to 6
- ffn_in: bfloat16 [512, 49, 128], P(('src', 'tgt')), may hold values from -6 to 6
- grad_out: bfloat16 [512, 49, 128], P(('src', 'tgt')), may hold values from -6 to 6
- ffn_up: bfloat16 [128, 512], replicated, may hold values from -0.5 to 0.5
- ffn_down: bfloat16 [512, 128], replicated, may hold values from -0.25 to 0.25
- so2_zero: bfloat16 [896, 1024], P('tgt'), may hold values from -0.1875 to 0.1875
- so2_one: bfloat16 [2, 768, 768], P(None, 'tgt'), may hold values from -0.15625 to 0.15625
- so2_two: bfloat16 [2, 640, 640], P(None, 'tgt'), may hold values from -0.15625 to 0.15625
- wigner: bfloat16 [64, 29, 49], replicated, may hold values from -1 to 1
- edge_src: int32 [32, 16, 128], P('src', 'tgt'), may hold values from 0 to 15
- edge_tgt: int32 [32, 16, 128], P('src', 'tgt'), may hold values from 0 to 31
- edge_angle: int32 [32, 16, 128], P('src', 'tgt'), may hold values from 0 to 63
- edge_radial: bfloat16 [32, 16, 128, 128], P('src', 'tgt'), may hold values from 0.25 to 2
- edge_count: int32 [32, 16], P('src', 'tgt'), may hold values from 1 to 128, as said below
Outputs:
- feat_grad: bfloat16 [512, 49, 128], P(('src', 'tgt'))
Inputs may be any that keep to these rules, and one draw needn't show every extreme that they name: The slots of a block at or past its edge_count are padding. Some block holds 128 edges.
All inputs are finite; a program needn't handle non-finite values.
Results may differ from a plain program's by a relative error of at most 0.006.
Values may be sent and summed in bfloat16 or wider, within the bound.
No kernel may reach another device: no remote copies, remote signals or barrier semaphores. Data moves between devices by JAX's collectives and lax.ppermute only.
A program may use at most 64 MiB of HBM per device.

v0:
```python
import math

import jax
import jax.numpy as jnp
import numpy as np
from jax import lax
from jax.experimental import pallas as pl
from jax.experimental.pallas import tpu as pltpu
from jax.sharding import Mesh
from jax.sharding import PartitionSpec as P

LMAX = 6
GRID_SIDE = 14
C = 128
KEEP = 29
COEF = 49
PAD = 56
message_scale = 0.125
BF = jnp.bfloat16
F32 = jnp.float32
VMEM = pltpu.VMEM
SHARE = 192
SENT = 248
AT_ONE, AT_TWO, AT_MORE, WHOLE = 896, 1664, 2304, 3072


def sphere_tables(degree_max, grid_side):
    polar_angle = (np.arange(grid_side) + 0.5) * np.pi / grid_side
    azimuth = np.arange(grid_side) * 2.0 * np.pi / grid_side
    cosine = np.cos(polar_angle)
    sine_theta = np.sin(polar_angle)
    coef_count = (degree_max + 1) * (degree_max + 1)
    harmonics = np.zeros((grid_side, grid_side, coef_count))
    for order_m in range(degree_max + 1):
        diagonal = np.ones(grid_side)
        for factor in range(1, order_m + 1):
            diagonal = diagonal * (2 * factor - 1) * sine_theta
        legendre = {order_m: diagonal}
        if order_m + 1 <= degree_max:
            legendre[order_m + 1] = cosine * (2 * order_m + 1) * diagonal
        for degree in range(order_m + 2, degree_max + 1):
            legendre[degree] = (
                (2 * degree - 1) * cosine * legendre[degree - 1]
                - (degree + order_m - 1) * legendre[degree - 2]
            ) / (degree - order_m)
        for degree in range(order_m, degree_max + 1):
            scaling = math.sqrt(
                (2 * degree + 1)
                / (4.0 * math.pi)
                * math.factorial(degree - order_m)
                / math.factorial(degree + order_m)
            )
            if order_m > 0:
                scaling = scaling * math.sqrt(2.0)
            polar_part = scaling * legendre[degree]
            centre = degree * degree + degree
            harmonics[:, :, centre + order_m] = (
                polar_part[:, None] * np.cos(order_m * azimuth)[None, :]
            )
            if order_m > 0:
                harmonics[:, :, centre - order_m] = (
                    polar_part[:, None] * np.sin(order_m * azimuth)[None, :]
                )
    to_grid = harmonics.reshape(grid_side * grid_side, coef_count)
    quadrature = np.repeat(sine_theta * (np.pi / grid_side) * (2.0 * np.pi / grid_side), grid_side)
    from_grid = (to_grid * quadrature[:, None]).T
    return to_grid.astype(np.float32), from_grid.astype(np.float32)


def dot(left, right):
    return jnp.dot(left, right, preferred_element_type=F32)


def dot_nt(left, right):
    return lax.dot_general(left, right, (((1,), (1,)), ((), ())), preferred_element_type=F32)


def pack_kernel(place, zero_ref, one_ref, two_ref, feat_ref, out_ref):
    for share in range(8):

        @pl.when(place[2] == share)
        def _():
            out_ref[0, 0:56, :] = zero_ref[:, 128 * share : 128 * share + 128]
            side, block = divmod(share, 6)
            out_ref[0, 56:104, :] = one_ref[side, :, 128 * block : 128 * block + 128]
            side, block = divmod(share, 5)
            out_ref[0, 104:144, :] = two_ref[side, :, 128 * block : 128 * block + 128]
            if share < 4:
                out_ref[0, 144:192, :] = one_ref[1, :, 128 * (share + 2) : 128 * (share + 3)]
            elif share < 6:
                out_ref[0, 144:184, :] = two_ref[1, :, 128 * (share - 1) : 128 * share]
                out_ref[0, 184:192, :] = jnp.zeros((8, C), BF)
            else:
                out_ref[0, 144:192, :] = jnp.zeros((48, C), BF)

    out_ref[0, SHARE : SHARE + COEF, :] = feat_ref[0]
    out_ref[0, SHARE + COEF : SENT, :] = jnp.zeros((PAD - COEF, C), BF)
    for peer in range(1, 16):
        out_ref[peer] = out_ref[0]


def pack_own(place, so2_zero, so2_one, so2_two, feat_in):
    return pl.pallas_call(
        pack_kernel,
        out_shape=jax.ShapeDtypeStruct((16, SENT, C), BF),
        in_specs=[pl.BlockSpec(memory_space=pltpu.SMEM)] + [pl.BlockSpec(memory_space=VMEM)] * 4,
        out_specs=pl.BlockSpec(memory_space=VMEM),
    )(place, so2_zero, so2_one, so2_two, feat_in)


def join_kernel(place, own_ref, other_ref, whole_ref, half_ref, feat_ref):
    core = place[0]
    share = place[2]

    def fill(side, ref, this_share):
        def pair(z_row, first, rows):
            return jnp.concatenate(
                [
                    ref[2 * z_row, first : first + rows, :],
                    ref[2 * z_row + 1, first : first + rows, :],
                ],
                axis=0,
            )

        def put(z_row, start, first, rows):
            block = pair(z_row, first, rows)
            at = start + 2 * rows * z_row
            whole_ref[side, at : at + 2 * rows, :] = block
            at = start // 2 + 2 * rows * (z_row % 4)

            @pl.when(core == z_row // 4)
            def _():
                half_ref[side, at : at + 2 * rows, :] = block

        for z_row in range(8):
            put(z_row, 0, 0, 56)
            put(z_row, AT_ONE, 56, 48)
            put(z_row, AT_TWO, 104, 40)

        @pl.when(this_share < 4)
        def _():
            for z_row in range(8):
                put(z_row, AT_MORE, 144, 48)

        @pl.when((this_share >= 4) & (this_share < 6))
        def _():
            for z_row in range(8):
                put(z_row, AT_MORE, 144, 40)

        @pl.when((this_share >= 6))
        def _():
            whole_ref[side, AT_MORE:WHOLE, :] = jnp.zeros((WHOLE - AT_MORE, C), BF)
            half_ref[side, AT_MORE // 2 : WHOLE // 2, :] = jnp.zeros(((WHOLE - AT_MORE) // 2, C), BF)

        @pl.when((this_share >= 4) & (this_share < 6))
        def _():
            whole_ref[side, AT_MORE + 640 : WHOLE, :] = jnp.zeros((128, C), BF)
            half_ref[side, AT_MORE // 2 + 320 : WHOLE // 2, :] = jnp.zeros((64, C), BF)

    fill(0, own_ref, share)
    fill(1, other_ref, share + 1 - 2 * core)
    for peer in range(16):
        feat_ref[peer] = own_ref[peer, SHARE:SENT, :]


def join_shares(place, own, other):
    vmem = pl.BlockSpec(memory_space=VMEM)
    return pl.pallas_call(
        join_kernel,
        out_shape=(
            jax.ShapeDtypeStruct((2, WHOLE, C), BF),
            jax.ShapeDtypeStruct((2, WHOLE // 2, C), BF),
            jax.ShapeDtypeStruct((16, PAD, C), BF),
        ),
        in_specs=[pl.BlockSpec(memory_space=pltpu.SMEM), vmem, vmem],
        out_specs=(vmem,) * 3,
    )(place, own, other)


def ffn_kernel(x_ref, g_ref, up_ref, down_ref, to_ref, from_ref, back_ref, out_ref, xs, gs):
    xs[0:COEF, :] = x_ref[0]
    xs[COEF:PAD, :] = jnp.zeros((PAD - COEF, C), BF)
    gs[0:COEF, :] = g_ref[0]
    gs[COEF:PAD, :] = jnp.zeros((PAD - COEF, C), BF)
    grid_feat = dot(to_ref[...], xs[...]).astype(BF)
    grad_value = dot(from_ref[...], gs[...]).astype(BF)
    pre_act = dot(grid_feat, up_ref[...])
    grad_act = dot_nt(grad_value, down_ref[...])
    gate = jax.nn.sigmoid(pre_act)
    grad_pre = (grad_act * gate * (1.0 + pre_act * (1.0 - gate))).astype(BF)
    grad_grid = dot_nt(grad_pre, up_ref[...]).astype(BF)
    out_ref[...] = (gs[...].astype(F32) + dot(back_ref[...], grad_grid)).astype(BF)


def ffn_backward(ffn_in, grad_out, ffn_up, ffn_down):
    to_grid, from_grid = sphere_tables(LMAX, GRID_SIDE)
    points = to_grid.shape[0]
    to_pad = np.zeros((208, PAD), np.float32)
    to_pad[:points, :COEF] = to_grid
    from_pad = np.zeros((208, PAD), np.float32)
    from_pad[:points, :COEF] = from_grid.T
    back_pad = np.ascontiguousarray(to_pad.T)
    tables = [jnp.asarray(table, F32).astype(BF) for table in (to_pad, from_pad, back_pad)]
    return pl.pallas_call(
        ffn_kernel,
        out_shape=jax.ShapeDtypeStruct((PAD, C), BF),
        in_specs=[pl.BlockSpec(memory_space=VMEM)] * 7,
        out_specs=pl.BlockSpec(memory_space=VMEM),
        scratch_shapes=[VMEM((PAD, C), BF), VMEM((PAD, C), BF)],
    )(ffn_in, grad_out, ffn_up, ffn_down, *tables)


def rotate_kernel(src, tgt, ang, feat_ref, grad_ref, wig_ref, rot_ref, go_ref, acc):
    slots = 128

    def body(step, carry):
        for lane in range(8):
            slot = step * 8 + lane
            rows = jnp.concatenate([feat_ref[src[slot]], grad_ref[tgt[slot]]], axis=1)
            turned = dot(wig_ref[ang[slot]], rows)
            acc[pl.ds(slot, 32, stride=slots), :] = turned[:, :C]
            go_ref[pl.ds(slot, 32, stride=slots), :] = turned[:, C:]
        return carry

    lax.fori_loop(0, slots // 8, body, 0)
    rot_ref[...] = acc[...].astype(BF)


def rotate_slots(src, tgt, ang, feat, grads, wig):
    smem = pl.BlockSpec(memory_space=pltpu.SMEM)
    vmem = pl.BlockSpec(memory_space=VMEM)
    return pl.pallas_call(
        rotate_kernel,
        out_shape=(
            jax.ShapeDtypeStruct((32 * 128, C), BF),
            jax.ShapeDtypeStruct((32 * 128, C), F32),
        ),
        in_specs=[smem] * 3 + [vmem] * 3,
        out_specs=(vmem, vmem),
        scratch_shapes=[VMEM((32 * 128, C), F32)],
    )(src, tgt, ang, feat, grads, wig)


def edge_kernel(
    place, src, ang, own_ref, near_ref, far_ref, half_ref, half_far_ref,
    rot_ref, go_ref, radial_ref, wig_ref, out_ref,
    w_zero, w_one, w_two, hidden, grad_rot, acc,
):
    core = place[0]
    quarter = place[1]

    def take(ref, at, ahead, side, half):
        share = 2 * lax.rem(quarter + ahead, 4) + side
        cut = 1 if half is None else 2

        def move(weight, block, first, rows):
            rows = rows // cut
            start = 0 if half is None else pl.multiple_of(rows * half, 64)
            weight[block, pl.ds(start, rows), :] = ref[at, first // cut : first // cut + rows, :]

        move(w_zero, share, 0, 896)
        move(w_one, share, AT_ONE, 768)
        move(w_two, share, AT_TWO, 640)

        @pl.when(share < 4)
        def _():
            move(w_one, 8 + share, AT_MORE, 768)

        @pl.when((share >= 4) & (share < 6))
        def _():
            move(w_two, 4 + share, AT_MORE, 640)

    for at in range(2):
        side = core if at == 0 else 1 - core
        take(own_ref, at, 0, side, None)
        take(near_ref, at, 3 - 2 * core, side, None)
        take(far_ref, at, 1 + 2 * core, 1 - side, None)
        take(half_ref, at, 2, side, core)
        take(half_far_ref, at, 2, 1 - side, 1 - core)

    def columns(weight, first, count, rows):
        return jnp.concatenate([weight[first + at, rows, :] for at in range(count)], axis=1)

    every = slice(None)

    def turned(first, count):
        return jnp.concatenate(
            [rot_ref[128 * row : 128 * row + 128, :] for row in range(first, first + count)], axis=1
        )

    radial = radial_ref[...].astype(F32)

    def put(first, rows, value):
        for row in range(rows):
            hidden[128 * (first + row) : 128 * (first + row) + 128, :] = (
                value[:, 128 * row : 128 * row + 128] * radial
            )

    left = turned(0, 7)
    for pair in range(4):
        put(2 * pair, 2, dot(left, columns(w_zero, 2 * pair, 2, every)))

    def higher(first, count, weight, hidden_first):
        plus = turned(first, count)
        minus = turned(first + count, count)
        both = jnp.concatenate(
            [jnp.concatenate([plus, -minus], axis=1), jnp.concatenate([minus, plus], axis=1)], axis=0
        )
        start = 0
        while start < count:
            wide = min(2, count - start)
            value = dot(
                both,
                jnp.concatenate(
                    [columns(weight, start, wide, every), columns(weight, count + start, wide, every)],
                    axis=0,
                ),
            )
            put(hidden_first + start, wide, value[:128])
            put(hidden_first + count + start, wide, value[128:])
            start = start + wide

    higher(7, 6, w_one, 8)
    higher(19, 5, w_two, 20)

    def hid(row):
        return hidden[128 * row : 128 * row + 128, :]

    def go(row):
        return go_ref[128 * row : 128 * row + 128, :] * message_scale

    scalar_pre = hid(0)
    sigmoid_scalar = jax.nn.sigmoid(scalar_pre)
    sigmoid_gate = jax.nn.sigmoid(hid(7))
    weight_gate = sigmoid_gate * radial
    grads = {}
    grads[0] = (
        go(0) * sigmoid_scalar * (1.0 + scalar_pre * (1.0 - sigmoid_scalar)) * radial
    ).astype(BF)
    total = jnp.zeros((128, C), F32)
    for kept in range(1, KEEP):
        row = kept if kept < 7 else kept + 1
        value = go(kept)
        total = total + value * hid(row)
        grads[row] = (value * weight_gate).astype(BF)
    grads[7] = (total * sigmoid_gate * (1.0 - sigmoid_gate) * radial).astype(BF)

    def side_by_side(first, count):
        return jnp.concatenate([grads[row] for row in range(first, first + count)], axis=1)

    def keep(first, value):
        for row in range(value.shape[1] // 128):
            grad_rot[128 * (first + row) : 128 * (first + row) + 128, :] = value[
                :, 128 * row : 128 * row + 128
            ]

    right = side_by_side(0, 8)
    for start in (0, 2, 4, 6):
        wide = min(2, 7 - start)
        rows = slice(128 * start, 128 * (start + wide))
        keep(start, dot_nt(right, columns(w_zero, 0, 8, rows)))

    def back(first, count, weight, hidden_first):
        both = jnp.concatenate(
            [side_by_side(hidden_first, count), side_by_side(hidden_first + count, count)], axis=0
        )
        start = 0
        while start < count:
            wide = min(2, count - start)
            rows = slice(128 * start, 128 * (start + wide))
            real = dot_nt(both, columns(weight, 0, count, rows))
            imag = dot_nt(both, columns(weight, count, count, rows))
            keep(first + start, real[:128] + imag[128:])
            keep(first + count + start, real[128:] - imag[:128])
            start = start + wide

    back(7, 6, w_one, 8)
    back(19, 5, w_two, 20)
    grad_rot[KEEP * 128 :, :] = jnp.zeros((3 * 128, C), F32)

    acc[...] = jnp.zeros_like(acc)
    live = place[3]

    def slot_body(step, carry):
        for lane in range(8):
            slot = step * 8 + lane
            rows = grad_rot[pl.ds(slot, 32, stride=128), :]
            rows = jnp.where(slot < live, rows, 0.0).astype(BF)
            acc[src[slot]] += dot(wig_ref[ang[slot]], rows)
        return carry

    lax.fori_loop(0, lax.div(live + 7, 8), slot_body, 0)
    out_ref[...] = acc[...].astype(BF)


def edge_backward(place, src, ang, shares, rot, go, radial, wig_back):
    smem = pl.BlockSpec(memory_space=pltpu.SMEM)
    vmem = pl.BlockSpec(memory_space=VMEM)
    return pl.pallas_call(
        edge_kernel,
        out_shape=jax.ShapeDtypeStruct((16, PAD, C), BF),
        in_specs=[smem] * 3 + [vmem] * 9,
        out_specs=vmem,
        scratch_shapes=[
            VMEM((8, 896, C), BF),
            VMEM((12, 768, C), BF),
            VMEM((10, 640, C), BF),
            VMEM((30 * 128, C), F32),
            VMEM((32 * 128, C), F32),
            VMEM((16, PAD, C), F32),
        ],
        compiler_params=pltpu.CompilerParams(vmem_limit_bytes=48 * 1024 * 1024),
    )(place, src, ang, *shares, rot, go, radial, wig_back)


def swap(value, axis):
    return lax.ppermute(value, axis, [(0, 1), (1, 0)])


def body(
    feat_in, ffn_in, grad_out, ffn_up, ffn_down, so2_zero, so2_one, so2_two, wigner,
    edge_src, edge_tgt, edge_angle, edge_radial, edge_count,
):
    core = lax.axis_index("core").astype(jnp.int32)
    x_here = lax.axis_index("x").astype(jnp.int32)
    y_hi = lax.axis_index("yhi").astype(jnp.int32)
    quarter = (x_here + 2 * y_hi) % 4
    place = jnp.stack([core, quarter, 2 * quarter + core, edge_count.reshape(())])

    sent = pack_own(place, so2_zero, so2_one, so2_two, feat_in)
    got = lax.all_to_all(sent, ("z", "ylo"), 0, 0, tiled=True)
    target_grad = ffn_backward(ffn_in, grad_out, ffn_up, ffn_down)
    grads = target_grad[None]
    for axis, mask in (("yhi", 2), ("yhi", 1), ("x", 2), ("x", 1), ("core", 1)):
        count = 2 if axis == "core" else 4
        other = lax.ppermute(grads, axis, [(at, at ^ mask) for at in range(count)])
        grads = jnp.concatenate([grads, other], axis=0)
    got_other = swap(got, "core")
    own, half, feat = join_shares(place, got, got_other)
    turn = [(2 * at, 2 * ((at + 1) % 4)) for at in range(4)]
    turn = turn + [(2 * at + 1, 2 * ((at + 3) % 4) + 1) for at in range(4)]
    near = lax.ppermute(own, ("x", "core"), turn)
    half_near = lax.ppermute(half, ("yhi", "core"), turn)
    far = swap(near, "core")
    half_far = swap(half_near, "core")
    shares = (own, near, far, half_near, half_far)

    src_slots = edge_src.reshape(-1)
    tgt_slots = edge_tgt.reshape(-1)
    angle_slots = edge_angle.reshape(-1)
    y_turn = (tgt_slots // 8) ^ y_hi
    x_turn = (tgt_slots // 2 % 4) ^ x_here
    core_turn = (tgt_slots % 2) ^ core
    tgt_piece = core_turn * 16 + x_turn % 2 * 8 + x_turn // 2 * 4 + y_turn % 2 * 2 + y_turn // 2
    wig = jnp.pad(wigner, ((0, 0), (0, 32 - KEEP), (0, PAD - COEF)))
    wig_back = jnp.transpose(wig, (0, 2, 1))
    rot, go = rotate_slots(src_slots, tgt_piece, angle_slots, feat, grads, wig)
    partial_sum = edge_backward(
        place, src_slots, angle_slots, shares, rot, go, edge_radial.reshape(128, C), wig_back
    )
    parts = lax.all_to_all(partial_sum, ("z", "ylo"), 0, 0, tiled=True)
    total = target_grad.astype(F32) + jnp.sum(parts.astype(F32), axis=0)
    return total[None, :COEF].astype(BF)


def solution(mesh):
    devices = mesh.devices.reshape(4, 4, 2, 8, 2)
    fine = Mesh(devices, ("yhi", "x", "core", "z", "ylo"))
    src = ("yhi", "x", "core")
    tgt = ("z", "ylo")
    placed = (
        P(src + tgt, None, None),
        P(src + tgt, None, None),
        P(src + tgt, None, None),
        P(),
        P(),
        P(tgt, None),
        P(None, tgt, None),
        P(None, tgt, None),
        P(),
        P(src, tgt, None),
        P(src, tgt, None),
        P(src, tgt, None),
        P(src, tgt, None, None),
        P(src, tgt),
    )
    return jax.shard_map(
        body,
        mesh=fine,
        in_specs=placed,
        out_specs=P(src + tgt, None, None),
        check_vma=False,
    )
```

profile of v0, /device:TPU:6, one launch (start us, length us, event | category | flops | bytes accessed | tf_op | source)
XLA Modules:
  0.0 153.5 jit_solution(3986019191140130687)
XLA Ops:
  1.2 2.2 %shard_map.164 = bf16[16,248,128]{2,1,0:T(8,128)(2,1)} custom-call(s32[4]{0:T(128)} %pad_add_fusion.place, bf16[56,1024]{1,0:T(8,128)(2,1)} %zero_ref.1, bf16[2,48,768]{2,1,0:T(8,128)(2,1)} %one_ref.1, bf16[2,40,640]{2,1,0:T(8,128)(2,1)} %two_ref.1, bf16[1,49,128]{2,1,0:T(8,128)(2,1)} %feat_ref.1), custom_call_target="tpu_custom_call" | custom-call | tf_op jit(solution)/shard_map/pallas_call | solution.py:103
  3.4 38.9 %all_to_all.10.own_ref = bf16[16,248,128]{2,1,0:T(8,128)(2,1)S(1)} all-to-all(bf16[16,248,128]{2,1,0:T(8,128)(2,1)} %shard_map.164), channel_id=1, replica_groups=mesh['yhi'=4,'x'=4,'core'=2,'z'=8,'ylo'=2] {'z','ylo'}, dimensions={0} | all-to-all | bytes 2031616 | tf_op jit(solution)/shard_map/all_to_all | solution.py:431
  42.4 1.9 %collective-permute-start = (bf16[16,248,128]{2,1,0:T(8,128)(2,1)S(1)}, bf16[16,248,128]{2,1,0:T(8,128)(2,1)S(1)}, u32[]{:S(2)}, u32[]{:S(2)}) collective-permute-start(bf16[16,248,128]{2,1,0:T(8,128)(2,1)S(1)} %all_to_all.10.own_ref), channel_id=1, source_target_pairs={{0,16},{16,0},{1,17},{17,1},{2,18},{18,2},{3,19},{19,3},{4,20},{20... | collective-permute-start | bytes 3047432 | tf_op jit(solution)/shard_map/ppermute | solution.py:417
  44.3 2.6 %collective-permute-done.other_ref = bf16[16,248,128]{2,1,0:T(8,128)(2,1)S(1)} collective-permute-done((bf16[16,248,128]{2,1,0:T(8,128)(2,1)S(1)}, bf16[16,248,128]{2,1,0:T(8,128)(2,1)S(1)}, u32[]{:S(2)}, u32[]{:S(2)}) %collective-permute-start) | collective-permute-done | bytes 1015840 | tf_op jit(solution)/shard_map/ppermute | solution.py:417
  46.9 1.0 copy-done.7
  47.8 3.5 %shard_map.165 = (bf16[2,3072,128]{2,1,0:T(8,128)(2,1)}, bf16[2,1536,128]{2,1,0:T(8,128)(2,1)}, bf16[16,56,128]{2,1,0:T(8,128)(2,1)}) custom-call(s32[4]{0:T(128)} %pad_add_fusion.place, bf16[16,248,128]{2,1,0:T(8,128)(2,1)} %copy-done.6, bf16[16,248,128]{2,1,0:T(8,128)(2,1)} %copy-done.7), custom_call_target="tpu_custom_call" | custom-call | tf_op jit(solution)/shard_map/pallas_call | solution.py:168
  51.3 2.4 %collective-permute-start.1 = (bf16[2,3072,128]{2,1,0:T(8,128)(2,1)}, bf16[2,3072,128]{2,1,0:T(8,128)(2,1)}, u32[]{:S(2)}, u32[]{:S(2)}) collective-permute-start(bf16[2,3072,128]{2,1,0:T(8,128)(2,1)} %get-tuple-element.10.own_ref), channel_id=1, source_target_pairs={{0,32},{32,64},{64,96},{96,0},{16,112},{48,16},{80,48},{112,80},{1... | collective-permute-start | bytes 4718600 | tf_op jit(solution)/shard_map/ppermute | solution.py:442
  53.7 4.5 %collective-permute-start.3 = (bf16[2,1536,128]{2,1,0:T(8,128)(2,1)}, bf16[2,1536,128]{2,1,0:T(8,128)(2,1)S(1)}, u32[]{:S(2)}, u32[]{:S(2)}) collective-permute-start(bf16[2,1536,128]{2,1,0:T(8,128)(2,1)} %get-tuple-element.11), channel_id=1, source_target_pairs={{0,128},{128,256},{256,384},{384,0},{16,400},{144,16},{272,144},{4... | collective-permute-start | bytes 2359304 | tf_op jit(solution)/shard_map/ppermute | solution.py:443
  58.2 15.7 %collective-permute-done.1.near_ref = bf16[2,3072,128]{2,1,0:T(8,128)(2,1)} collective-permute-done((bf16[2,3072,128]{2,1,0:T(8,128)(2,1)}, bf16[2,3072,128]{2,1,0:T(8,128)(2,1)}, u32[]{:S(2)}, u32[]{:S(2)}) %collective-permute-start.1) | collective-permute-done | bytes 1572896 | tf_op jit(solution)/shard_map/ppermute | solution.py:442
  73.9 2.1 %collective-permute-start.2 = (bf16[2,3072,128]{2,1,0:T(8,128)(2,1)}, bf16[2,3072,128]{2,1,0:T(8,128)(2,1)}, u32[]{:S(2)}, u32[]{:S(2)}) collective-permute-start(bf16[2,3072,128]{2,1,0:T(8,128)(2,1)} %collective-permute-done.1.near_ref), channel_id=1, source_target_pairs={{0,16},{16,0},{1,17},{17,1},{2,18},{18,2},{3,19},{19,3},{4,20},{20... | collective-permute-start | bytes 4718600 | tf_op jit(solution)/shard_map/ppermute | solution.py:417
  76.0 2.4 %shard_map.163 = bf16[56,128]{1,0:T(8,128)(2,1)} custom-call(bf16[1,49,128]{2,1,0:T(8,128)(2,1)} %x_ref.1, bf16[1,49,128]{2,1,0:T(8,128)(2,1)} %g_ref.1, bf16[128,512]{1,0:T(8,128)(2,1)} %up_ref.1, bf16[512,128]{1,0:T(8,128)(2,1)} %down_ref.1, bf16[208,56]{1,0:T(8,128)(2,1)} %constant.125.to_ref, bf16[208,56]{1,0:T(8,128)(2,1)} %constant.126.from_ref, ...), custom_call_target="tpu_custom_call" | custom-call | tf_op jit(solution)/shard_map/pallas_call | solution.py:204
  78.4 7.1 %collective-permute-start.5 = (bf16[1,56,128]{2,1,0:T(8,128)(2,1)}, bf16[1,56,128]{2,1,0:T(8,128)(2,1)S(1)}, u32[]{:S(2)}, u32[]{:S(2)}) collective-permute-start(bf16[1,56,128]{2,1,0:T(8,128)(2,1)} %bitcast.36), channel_id=1, source_target_pairs={{0,256},{128,384},{256,0},{384,128},{1,257},{129,385},{257,1},{385... | collective-permute-start | bytes 43016 | tf_op jit(solution)/shard_map/ppermute | solution.py:436
  85.5 1.3 constant_dynamic-update-slice_fusion.4
  86.9 1.6 %copy.18 = bf16[64,29,49]{1,2,0:T(8,128)(2,1)S(1)} copy(bf16[64,29,49]{0,1,2:T(8,128)(2,1)} %param.25) | data formatting | bytes 363776 | tf_op args[8]
  88.4 0.7 pad_maximum_fusion.2
  89.2 4.3 %collective-permute-start.6 = (bf16[2,56,128]{2,1,0:T(8,128)(2,1)S(1)}, bf16[2,56,128]{2,1,0:T(8,128)(2,1)S(1)}, u32[]{:S(2)}, u32[]{:S(2)}) collective-permute-start(bf16[2,56,128]{2,1,0:T(8,128)(2,1)S(1)} %pad_maximum_fusion.2), channel_id=1, source_target_pairs={{0,128},{128,0},{256,384},{384,256},{1,129},{129,1},{257,385},{385... | collective-permute-start | bytes 86024 | tf_op jit(solution)/shard_map/ppermute | solution.py:436
  94.1 1.9 %collective-permute-done.6 = bf16[2,56,128]{2,1,0:T(8,128)(2,1)S(1)} collective-permute-done((bf16[2,56,128]{2,1,0:T(8,128)(2,1)S(1)}, bf16[2,56,128]{2,1,0:T(8,128)(2,1)S(1)}, u32[]{:S(2)}, u32[]{:S(2)}) %collective-permute-start.6) | collective-permute-done | bytes 28704 | tf_op jit(solution)/shard_map/ppermute | solution.py:436
  96.0 0.7 pad_maximum_fusion.1
  96.7 2.8 %collective-permute-start.7 = (bf16[4,56,128]{2,1,0:T(8,128)(2,1)S(1)}, bf16[4,56,128]{2,1,0:T(8,128)(2,1)S(1)}, u32[]{:S(2)}, u32[]{:S(2)}) collective-permute-start(bf16[4,56,128]{2,1,0:T(8,128)(2,1)S(1)} %pad_maximum_fusion.1), channel_id=1, source_target_pairs={{0,64},{32,96},{64,0},{96,32},{1,65},{33,97},{65,1},{97,33},{2,66}... | collective-permute-start | bytes 172040 | tf_op jit(solution)/shard_map/ppermute | solution.py:436
  100.1 1.9 %collective-permute-start.4 = (bf16[2,1536,128]{2,1,0:T(8,128)(2,1)S(1)}, bf16[2,1536,128]{2,1,0:T(8,128)(2,1)}, u32[]{:S(2)}, u32[]{:S(2)}) collective-permute-start(bf16[2,1536,128]{2,1,0:T(8,128)(2,1)S(1)} %collective-permute-done.3.half_ref), channel_id=1, source_target_pairs={{0,16},{16,0},{1,17},{17,1},{2,18},{18,2},{3,19},{19,3},{4,20},{20... | collective-permute-start | bytes 2359304 | tf_op jit(solution)/shard_map/ppermute | solution.py:417
  102.0 2.2 %collective-permute-done.7 = bf16[4,56,128]{2,1,0:T(8,128)(2,1)S(1)} collective-permute-done((bf16[4,56,128]{2,1,0:T(8,128)(2,1)S(1)}, bf16[4,56,128]{2,1,0:T(8,128)(2,1)S(1)}, u32[]{:S(2)}, u32[]{:S(2)}) %collective-permute-start.7) | collective-permute-done | bytes 57376 | tf_op jit(solution)/shard_map/ppermute | solution.py:436
  104.3 2.2 %collective-permute-start.8 = (bf16[8,56,128]{2,1,0:T(8,128)(2,1)S(1)}, bf16[8,56,128]{2,1,0:T(8,128)(2,1)S(1)}, u32[]{:S(2)}, u32[]{:S(2)}) collective-permute-start(bf16[8,56,128]{2,1,0:T(8,128)(2,1)S(1)} %pad_maximum_fusion), channel_id=1, source_target_pairs={{0,32},{32,0},{64,96},{96,64},{1,33},{33,1},{65,97},{97,65},{2,34}... | collective-permute-start | bytes 344072 | tf_op jit(solution)/shard_map/ppermute | solution.py:436
  107.2 3.8 %collective-permute-done.8 = bf16[8,56,128]{2,1,0:T(8,128)(2,1)S(1)} collective-permute-done((bf16[8,56,128]{2,1,0:T(8,128)(2,1)S(1)}, bf16[8,56,128]{2,1,0:T(8,128)(2,1)S(1)}, u32[]{:S(2)}, u32[]{:S(2)}) %collective-permute-start.8) | collective-permute-done | bytes 114720 | tf_op jit(solution)/shard_map/ppermute | solution.py:436
  111.0 0.7 constant_dynamic-update-slice_fusion
  111.6 1.9 %collective-permute-start.9 = (bf16[16,56,128]{2,1,0:T(8,128)(2,1)}, bf16[16,56,128]{2,1,0:T(8,128)(2,1)}, u32[]{:S(2)}, u32[]{:S(2)}) collective-permute-start(bf16[16,56,128]{2,1,0:T(8,128)(2,1)} %get-tuple-element.15), channel_id=1, source_target_pairs={{0,16},{16,0},{1,17},{17,1},{2,18},{18,2},{3,19},{19,3},{4,20},{20... | collective-permute-start | bytes 688136 | tf_op jit(solution)/shard_map/ppermute | solution.py:436
  113.8 1.3 copy.20
  115.1 2.1 %pad.4.clone.wig_ref = bf16[64,32,56]{2,1,0:T(8,128)(2,1)} pad(bf16[64,29,49]{2,1,0:T(8,128)(2,1)} %copy.20, bf16[]{:T(256)} %constant.108.clone.1), padding=0_0x0_3x0_7 | pad | bytes 411266 | tf_op jit(solution)/shard_map/jit(_pad)/pad | solution.py:455
  117.8 1.6 %constant_dynamic-update-slice_fusion.5.grad_ref = bf16[32,56,128]{2,1,0:T(8,128)(2,1)} fusion(bf16[32,56,128]{2,1,0:T(8,128)(2,1)} %copy-done.9, bf16[16,56,128]{2,1,0:T(8,128)(2,1)} %collective-permute-done.9), kind=kLoop, calls=%fused_computation.11 | loop fusion | bytes 458752 | tf_op jit(solution)/shard_map/concatenate | solution.py:437
  119.4 8.5 %shard_map.166 = (bf16[4096,128]{1,0:T(8,128)(2,1)}, f32[4096,128]{1,0:T(8,128)}) custom-call(s32[128]{0:T(128)} %bitcast.32, s32[128]{0:T(128)} %fusion.10.tgt, s32[128]{0:T(128)} %bitcast.34, bf16[16,56,128]{2,1,0:T(8,128)(2,1)} %get-tuple-element.12.feat_ref, bf16[32,56,128]{2,1,0:T(8,128)(2,1)} %constant_dynamic-update-slice_fusion.5.grad_ref, ...), custom_call_target="tpu_custom_call" | custom-call | tf_op jit(solution)/shard_map/pallas_call | solution.py:232
  128.0 1.2 copy-done.1
  129.2 10.2 %shard_map.167 = bf16[16,56,128]{2,1,0:T(8,128)(2,1)S(1)} custom-call(s32[4]{0:T(128)S(1)} %copy-done.3, s32[128]{0:T(128)S(1)} %bitcast.33, s32[128]{0:T(128)S(1)} %bitcast.35, bf16[2,3072,128]{2,1,0:T(8,128)(2,1)S(1)} %copy-done, bf16[2,3072,128]{2,1,0:T(8,128)(2,1)} %collective-permute-done.1.near_ref, ...), custom_call_target="tpu_custom_call" | custom-call | tf_op jit(solution)/shard_map/pallas_call | solution.py:399
  139.5 13.4 %all_to_all.11 = bf16[16,56,128]{2,1,0:T(8,128)(2,1)S(1)} all-to-all(bf16[16,56,128]{2,1,0:T(8,128)(2,1)S(1)} %shard_map.167), channel_id=1, replica_groups=mesh['yhi'=4,'x'=4,'core'=2,'z'=8,'ylo'=2] {'z','ylo'}, dimensions={0} | all-to-all | bytes 458752 | tf_op jit(solution)/shard_map/all_to_all | solution.py:461
  (34 shorter events, 3.9 us)
Async XLA Ops:
  42.4 4.5 %copy-start.6 = (bf16[16,248,128]{2,1,0:T(8,128)(2,1)}, bf16[16,248,128]{2,1,0:T(8,128)(2,1)S(1)}, u32[]{:S(2)}) copy-start(bf16[16,248,128]{2,1,0:T(8,128)(2,1)S(1)} %all_to_all.10.own_ref) | copy-start | bytes 3047428
  42.4 4.5 %collective-permute-start = (bf16[16,248,128]{2,1,0:T(8,128)(2,1)S(1)}, bf16[16,248,128]{2,1,0:T(8,128)(2,1)S(1)}, u32[]{:S(2)}, u32[]{:S(2)}) collective-permute-start(bf16[16,248,128]{2,1,0:T(8,128)(2,1)S(1)} %all_to_all.10.own_ref), channel_id=1, source_target_pairs={{0,16},{16,0},{1,17},{17,1},{2,18},{18,2},{3,19},{19,3},{4,20},{20... | collective-permute-start | bytes 3047432 | tf_op jit(solution)/shard_map/ppermute | solution.py:417
  46.9 1.0 copy-start.7
  51.3 22.6 %collective-permute-start.1 = (bf16[2,3072,128]{2,1,0:T(8,128)(2,1)}, bf16[2,3072,128]{2,1,0:T(8,128)(2,1)}, u32[]{:S(2)}, u32[]{:S(2)}) collective-permute-start(bf16[2,3072,128]{2,1,0:T(8,128)(2,1)} %get-tuple-element.10.own_ref), channel_id=1, source_target_pairs={{0,32},{32,64},{64,96},{96,0},{16,112},{48,16},{80,48},{112,80},{1... | collective-permute-start | bytes 4718600 | tf_op jit(solution)/shard_map/ppermute | solution.py:442
  53.7 46.4 %collective-permute-start.3 = (bf16[2,1536,128]{2,1,0:T(8,128)(2,1)}, bf16[2,1536,128]{2,1,0:T(8,128)(2,1)S(1)}, u32[]{:S(2)}, u32[]{:S(2)}) collective-permute-start(bf16[2,1536,128]{2,1,0:T(8,128)(2,1)} %get-tuple-element.11), channel_id=1, source_target_pairs={{0,128},{128,256},{256,384},{384,0},{16,400},{144,16},{272,144},{4... | collective-permute-start | bytes 2359304 | tf_op jit(solution)/shard_map/ppermute | solution.py:443
  73.9 54.0 %collective-permute-start.2 = (bf16[2,3072,128]{2,1,0:T(8,128)(2,1)}, bf16[2,3072,128]{2,1,0:T(8,128)(2,1)}, u32[]{:S(2)}, u32[]{:S(2)}) collective-permute-start(bf16[2,3072,128]{2,1,0:T(8,128)(2,1)} %collective-permute-done.1.near_ref), channel_id=1, source_target_pairs={{0,16},{16,0},{1,17},{17,1},{2,18},{18,2},{3,19},{19,3},{4,20},{20... | collective-permute-start | bytes 4718600 | tf_op jit(solution)/shard_map/ppermute | solution.py:417
  78.4 25.9 %copy-start.8 = (bf16[56,128]{1,0:T(8,128)(2,1)S(1)}, bf16[56,128]{1,0:T(8,128)(2,1)}, u32[]{:S(2)}) copy-start(bf16[56,128]{1,0:T(8,128)(2,1)} %shard_map.163) | copy-start | bytes 43012
  78.4 10.0 %collective-permute-start.5 = (bf16[1,56,128]{2,1,0:T(8,128)(2,1)}, bf16[1,56,128]{2,1,0:T(8,128)(2,1)S(1)}, u32[]{:S(2)}, u32[]{:S(2)}) collective-permute-start(bf16[1,56,128]{2,1,0:T(8,128)(2,1)} %bitcast.36), channel_id=1, source_target_pairs={{0,256},{128,384},{256,0},{384,128},{1,257},{129,385},{257,1},{385... | collective-permute-start | bytes 43016 | tf_op jit(solution)/shard_map/ppermute | solution.py:436
  89.2 6.8 %collective-permute-start.6 = (bf16[2,56,128]{2,1,0:T(8,128)(2,1)S(1)}, bf16[2,56,128]{2,1,0:T(8,128)(2,1)S(1)}, u32[]{:S(2)}, u32[]{:S(2)}) collective-permute-start(bf16[2,56,128]{2,1,0:T(8,128)(2,1)S(1)} %pad_maximum_fusion.2), channel_id=1, source_target_pairs={{0,128},{128,0},{256,384},{384,256},{1,129},{129,1},{257,385},{385... | collective-permute-start | bytes 86024 | tf_op jit(solution)/shard_map/ppermute | solution.py:436
  96.7 7.6 %collective-permute-start.7 = (bf16[4,56,128]{2,1,0:T(8,128)(2,1)S(1)}, bf16[4,56,128]{2,1,0:T(8,128)(2,1)S(1)}, u32[]{:S(2)}, u32[]{:S(2)}) collective-permute-start(bf16[4,56,128]{2,1,0:T(8,128)(2,1)S(1)} %pad_maximum_fusion.1), channel_id=1, source_target_pairs={{0,64},{32,96},{64,0},{96,32},{1,65},{33,97},{65,1},{97,33},{2,66}... | collective-permute-start | bytes 172040 | tf_op jit(solution)/shard_map/ppermute | solution.py:436
  100.1 27.8 %collective-permute-start.4 = (bf16[2,1536,128]{2,1,0:T(8,128)(2,1)S(1)}, bf16[2,1536,128]{2,1,0:T(8,128)(2,1)}, u32[]{:S(2)}, u32[]{:S(2)}) collective-permute-start(bf16[2,1536,128]{2,1,0:T(8,128)(2,1)S(1)} %collective-permute-done.3.half_ref), channel_id=1, source_target_pairs={{0,16},{16,0},{1,17},{17,1},{2,18},{18,2},{3,19},{19,3},{4,20},{20... | collective-permute-start | bytes 2359304 | tf_op jit(solution)/shard_map/ppermute | solution.py:417
  104.3 6.7 %collective-permute-start.8 = (bf16[8,56,128]{2,1,0:T(8,128)(2,1)S(1)}, bf16[8,56,128]{2,1,0:T(8,128)(2,1)S(1)}, u32[]{:S(2)}, u32[]{:S(2)}) collective-permute-start(bf16[8,56,128]{2,1,0:T(8,128)(2,1)S(1)} %pad_maximum_fusion), channel_id=1, source_target_pairs={{0,32},{32,0},{64,96},{96,64},{1,33},{33,1},{65,97},{97,65},{2,34}... | collective-permute-start | bytes 344072 | tf_op jit(solution)/shard_map/ppermute | solution.py:436
  111.6 2.1 %copy-start.9 = (bf16[32,56,128]{2,1,0:T(8,128)(2,1)}, bf16[32,56,128]{2,1,0:T(8,128)(2,1)S(1)}, u32[]{:S(2)}) copy-start(bf16[32,56,128]{2,1,0:T(8,128)(2,1)S(1)} %get-tuple-element.16) | copy-start | bytes 1376260
  111.6 6.2 %collective-permute-start.9 = (bf16[16,56,128]{2,1,0:T(8,128)(2,1)}, bf16[16,56,128]{2,1,0:T(8,128)(2,1)}, u32[]{:S(2)}, u32[]{:S(2)}) collective-permute-start(bf16[16,56,128]{2,1,0:T(8,128)(2,1)} %get-tuple-element.15), channel_id=1, source_target_pairs={{0,16},{16,0},{1,17},{17,1},{2,18},{18,2},{3,19},{19,3},{4,20},{20... | collective-permute-start | bytes 688136 | tf_op jit(solution)/shard_map/ppermute | solution.py:436
  113.7 3.5 %copy-start.10 = (s32[1,1,128]{2,1,0:T(1,128)S(1)}, s32[1,1,128]{2,1,0:T(1,128)}, u32[]{:S(2)}) copy-start(s32[1,1,128]{2,1,0:T(1,128)} %param.27) | copy-start | bytes 1540
  115.1 12.9 %copy-start = (bf16[2,3072,128]{2,1,0:T(8,128)(2,1)S(1)}, bf16[2,3072,128]{2,1,0:T(8,128)(2,1)}, u32[]{:S(2)}) copy-start(bf16[2,3072,128]{2,1,0:T(8,128)(2,1)} %get-tuple-element.10.own_ref) | copy-start | bytes 4718596
  115.1 12.9 %copy-start.2 = (bf16[1,1,128,128]{3,2,1,0:T(8,128)(2,1)S(1)}, bf16[1,1,128,128]{3,2,1,0:T(8,128)(2,1)}, u32[]{:S(2)}) copy-start(bf16[1,1,128,128]{3,2,1,0:T(8,128)(2,1)} %param.29) | copy-start | bytes 98308
  115.1 12.9 %copy-start.3 = (s32[4]{0:T(128)S(1)}, s32[4]{0:T(128)}, u32[]{:S(2)}) copy-start(s32[4]{0:T(128)} %pad_add_fusion.place) | copy-start | bytes 52
  115.1 12.9 %copy-start.4 = (s32[1,1,128]{2,1,0:T(1,128)S(1)}, s32[1,1,128]{2,1,0:T(1,128)}, u32[]{:S(2)}) copy-start(s32[1,1,128]{2,1,0:T(1,128)} %param.26) | copy-start | bytes 1540
  115.1 12.9 %copy-start.5 = (s32[1,1,128]{2,1,0:T(1,128)S(1)}, s32[1,1,128]{2,1,0:T(1,128)}, u32[]{:S(2)}) copy-start(s32[1,1,128]{2,1,0:T(1,128)} %param.28) | copy-start | bytes 1540
  128.0 1.2 copy-start.1
where the time goes:
time: 157 us; the launch traced here: 154 us
  blocking collectives  52.4 us (33%)
  starting transfers between devices  31.3 us (20%)
  Pallas kernels  26.8 us (17%)
  waiting for transfers between devices  26.1 us (17%)
  local copies, waits for them, and re-layouts  12.9 us (8%)
  other arithmetic  3.22 us (2%)
    all_to_all x1, blocking collectives, body(): got = lax.all_to_all(sent, ('z', 'ylo'), 0, 0, tiled=True)  38.9 us
    ppermute x5, starting transfers between devices, body(): other = lax.ppermute(grads, axis, [(at, at ^ mask) for at in range(count)])  18.5 us
    ppermute x1, waiting for transfers between devices, body(): near = lax.ppermute(own, ('x', 'core'), turn)  15.7 us
    all_to_all x1, blocking collectives, body(): parts = lax.all_to_all(partial_sum, ('z', 'ylo'), 0, 0, tiled=True)  13.4 us
    pallas_call x1, Pallas kernels, edge_backward(): pl.pallas_call(edge_kernel, out_shape=jax.ShapeDtypeStruct((16, PAD, C),...  10.2 us
    pallas_call x1, Pallas kernels, rotate_slots(): pl.pallas_call(rotate_kernel, out_shape=(jax.ShapeDtypeStruct((32 * 128,...  8.54 us
    unnamed x28, local copies, waits for them, and re-layouts  8.29 us
    ppermute x5, waiting for transfers between devices, body(): other = lax.ppermute(grads, axis, [(at, at ^ mask) for at in range(count)])  7.85 us
  transfers between devices with their start and end apart: 10, of which 5 were waited for; matrix products, arithmetic and copies ran while one was open for 8% of the time, Pallas kernels for 7%

commit v1 on v0

--- a/solution.py
+++ b/solution.py
@@ -67,6 +67,10 @@
     return to_grid.astype(np.float32), from_grid.astype(np.float32)
 
 
+def grant(mebibytes):
+    return pltpu.CompilerParams(vmem_limit_bytes=mebibytes * 1024 * 1024)
+
+
 def dot(left, right):
     return jnp.dot(left, right, preferred_element_type=F32)
 
@@ -75,7 +79,11 @@
     return lax.dot_general(left, right, (((1,), (1,)), ((), ())), preferred_element_type=F32)
 
 
-def pack_kernel(place, zero_ref, one_ref, two_ref, feat_ref, out_ref):
+def pack_kernel(place, zero_ref, one_ref, two_ref, feat_ref, x_ref, g_ref, out_ref, pair_ref):
+    for row, ref in ((0, x_ref), (1, g_ref)):
+        pair_ref[row, 0:COEF, :] = ref[0]
+        pair_ref[row, COEF:PAD, :] = jnp.zeros((PAD - COEF, C), BF)
+
     for share in range(8):
 
         @pl.when(place[2] == share)
@@ -99,13 +107,18 @@
         out_ref[peer] = out_ref[0]
 
 
-def pack_own(place, so2_zero, so2_one, so2_two, feat_in):
+def pack_own(place, so2_zero, so2_one, so2_two, feat_in, ffn_in, grad_out):
+    vmem = pl.BlockSpec(memory_space=VMEM)
     return pl.pallas_call(
         pack_kernel,
-        out_shape=jax.ShapeDtypeStruct((16, SENT, C), BF),
-        in_specs=[pl.BlockSpec(memory_space=pltpu.SMEM)] + [pl.BlockSpec(memory_space=VMEM)] * 4,
-        out_specs=pl.BlockSpec(memory_space=VMEM),
-    )(place, so2_zero, so2_one, so2_two, feat_in)
+        out_shape=(
+            jax.ShapeDtypeStruct((16, SENT, C), BF),
+            jax.ShapeDtypeStruct((2, PAD, C), BF),
+        ),
+        in_specs=[pl.BlockSpec(memory_space=pltpu.SMEM)] + [vmem] * 6,
+        out_specs=(vmem, vmem),
+        compiler_params=grant(16),
+    )(place, so2_zero, so2_one, so2_two, feat_in, ffn_in, grad_out)
 
 
 def join_kernel(place, own_ref, other_ref, whole_ref, half_ref, feat_ref):
@@ -174,25 +187,25 @@
         ),
         in_specs=[pl.BlockSpec(memory_space=pltpu.SMEM), vmem, vmem],
         out_specs=(vmem,) * 3,
+        compiler_params=grant(16),
     )(place, own, other)
 
 
-def ffn_kernel(x_ref, g_ref, up_ref, down_ref, to_ref, from_ref, back_ref, out_ref, xs, gs):
-    xs[0:COEF, :] = x_ref[0]
-    xs[COEF:PAD, :] = jnp.zeros((PAD - COEF, C), BF)
-    gs[0:COEF, :] = g_ref[0]
-    gs[COEF:PAD, :] = jnp.zeros((PAD - COEF, C), BF)
-    grid_feat = dot(to_ref[...], xs[...]).astype(BF)
-    grad_value = dot(from_ref[...], gs[...]).astype(BF)
-    pre_act = dot(grid_feat, up_ref[...])
-    grad_act = dot_nt(grad_value, down_ref[...])
-    gate = jax.nn.sigmoid(pre_act)
-    grad_pre = (grad_act * gate * (1.0 + pre_act * (1.0 - gate))).astype(BF)
-    grad_grid = dot_nt(grad_pre, up_ref[...]).astype(BF)
-    out_ref[...] = (gs[...].astype(F32) + dot(back_ref[...], grad_grid)).astype(BF)
-
-
-def ffn_backward(ffn_in, grad_out, ffn_up, ffn_down):
+def ffn_kernel(own_ref, other_ref, up_ref, down_ref, to_ref, from_ref, back_ref, spread_ref):
+    for place, ref in ((0, own_ref), (1, other_ref)):
+        grid_feat = dot(to_ref[...], ref[0]).astype(BF)
+        grad_value = dot(from_ref[...], ref[1]).astype(BF)
+        pre_act = dot(grid_feat, up_ref[...])
+        grad_act = dot_nt(grad_value, down_ref[...])
+        gate = jax.nn.sigmoid(pre_act)
+        grad_pre = (grad_act * gate * (1.0 + pre_act * (1.0 - gate))).astype(BF)
+        grad_grid = dot_nt(grad_pre, up_ref[...]).astype(BF)
+        result = (ref[1].astype(F32) + dot(back_ref[...], grad_grid)).astype(BF)
+        for peer in range(16):
+            spread_ref[peer, place] = result
+
+
+def ffn_backward(own, other, ffn_up, ffn_down):
     to_grid, from_grid = sphere_tables(LMAX, GRID_SIDE)
     points = to_grid.shape[0]
     to_pad = np.zeros((208, PAD), np.float32)
@@ -203,11 +216,11 @@
     tables = [jnp.asarray(table, F32).astype(BF) for table in (to_pad, from_pad, back_pad)]
     return pl.pallas_call(
         ffn_kernel,
-        out_shape=jax.ShapeDtypeStruct((PAD, C), BF),
+        out_shape=jax.ShapeDtypeStruct((16, 2, PAD, C), BF),
         in_specs=[pl.BlockSpec(memory_space=VMEM)] * 7,
         out_specs=pl.BlockSpec(memory_space=VMEM),
-        scratch_shapes=[VMEM((PAD, C), BF), VMEM((PAD, C), BF)],
-    )(ffn_in, grad_out, ffn_up, ffn_down, *tables)
+        compiler_params=grant(16),
+    )(own, other, ffn_up, ffn_down, *tables)
 
 
 def rotate_kernel(src, tgt, ang, feat_ref, grad_ref, wig_ref, rot_ref, go_ref, acc):
@@ -238,45 +251,62 @@
         in_specs=[smem] * 3 + [vmem] * 3,
         out_specs=(vmem, vmem),
         scratch_shapes=[VMEM((32 * 128, C), F32)],
+        compiler_params=grant(16),
     )(src, tgt, ang, feat, grads, wig)
 
 
 def edge_kernel(
     place, src, ang, own_ref, near_ref, far_ref, half_ref, half_far_ref,
     rot_ref, go_ref, radial_ref, wig_ref, out_ref,
-    w_zero, w_one, w_two, hidden, grad_rot, acc,
+    w_zero, w_one, w_two, hidden, grad_rot, acc, sems,
 ):
     core = place[0]
     quarter = place[1]
-
-    def take(ref, at, ahead, side, half):
+    copies = ([], [], [])
+
+    def take(number, ref, at, ahead, side, half):
         share = 2 * lax.rem(quarter + ahead, 4) + side
         cut = 1 if half is None else 2
 
-        def move(weight, block, first, rows):
+        def move(weight, block, first, rows, part):
             rows = rows // cut
             start = 0 if half is None else pl.multiple_of(rows * half, 64)
-            weight[block, pl.ds(start, rows), :] = ref[at, first // cut : first // cut + rows, :]
-
-        move(w_zero, share, 0, 896)
-        move(w_one, share, AT_ONE, 768)
-        move(w_two, share, AT_TWO, 640)
-
-        @pl.when(share < 4)
-        def _():
-            move(w_one, 8 + share, AT_MORE, 768)
-
-        @pl.when((share >= 4) & (share < 6))
-        def _():
-            move(w_two, 4 + share, AT_MORE, 640)
-
+            return pltpu.make_async_copy(
+                ref.at[at, pl.ds(first // cut, rows), :],
+                weight.at[block, pl.ds(start, rows), :],
+                sems.at[number, part],
+            )
+
+        extra_one = share < 4
+        extra_two = (share >= 4) & (share < 6)
+        copies[0].append((None, lambda: move(w_zero, share, 0, 896, 0)))
+        copies[1].append((None, lambda: move(w_one, share, AT_ONE, 768, 1)))
+        copies[2].append((None, lambda: move(w_two, share, AT_TWO, 640, 2)))
+        copies[1].append((extra_one, lambda: move(w_one, 8 + share, AT_MORE, 768, 3)))
+        copies[2].append((extra_two, lambda: move(w_two, 4 + share, AT_MORE, 640, 3)))
+
+    number = 0
     for at in range(2):
         side = core if at == 0 else 1 - core
-        take(own_ref, at, 0, side, None)
-        take(near_ref, at, 3 - 2 * core, side, None)
-        take(far_ref, at, 1 + 2 * core, 1 - side, None)
-        take(half_ref, at, 2, side, core)
-        take(half_far_ref, at, 2, 1 - side, 1 - core)
+        for ref, ahead, its_side, half in (
+            (own_ref, 0, side, None),
+            (near_ref, 3 - 2 * core, side, None),
+            (far_ref, 1 + 2 * core, 1 - side, None),
+            (half_ref, 2, side, core),
+            (half_far_ref, 2, 1 - side, 1 - core),
+        ):
+            take(number, ref, at, ahead, its_side, half)
+            number = number + 1
+
+    def each(group, act):
+        for condition, make in copies[group]:
+            if condition is None:
+                act(make())
+            else:
+                pl.when(condition)(lambda make=make: act(make()))
+
+    for group in range(3):
+        each(group, lambda copy: copy.start())
 
     def columns(weight, first, count, rows):
         return jnp.concatenate([weight[first + at, rows, :] for at in range(count)], axis=1)
@@ -296,6 +326,7 @@
                 value[:, 128 * row : 128 * row + 128] * radial
             )
 
+    each(0, lambda copy: copy.wait())
     left = turned(0, 7)
     for pair in range(4):
         put(2 * pair, 2, dot(left, columns(w_zero, 2 * pair, 2, every)))
@@ -320,7 +351,9 @@
             put(hidden_first + count + start, wide, value[128:])
             start = start + wide
 
+    each(1, lambda copy: copy.wait())
     higher(7, 6, w_one, 8)
+    each(2, lambda copy: copy.wait())
     higher(19, 5, w_two, 20)
 
     def hid(row):
@@ -399,7 +432,7 @@
     return pl.pallas_call(
         edge_kernel,
         out_shape=jax.ShapeDtypeStruct((16, PAD, C), BF),
-        in_specs=[smem] * 3 + [vmem] * 9,
+        in_specs=[smem] * 3 + [pl.BlockSpec(memory_space=pl.ANY)] * 5 + [vmem] * 4,
         out_specs=vmem,
         scratch_shapes=[
             VMEM((8, 896, C), BF),
@@ -408,8 +441,9 @@
             VMEM((30 * 128, C), F32),
             VMEM((32 * 128, C), F32),
             VMEM((16, PAD, C), F32),
+            pltpu.SemaphoreType.DMA((10, 4)),
         ],
-        compiler_params=pltpu.CompilerParams(vmem_limit_bytes=48 * 1024 * 1024),
+        compiler_params=grant(28),
     )(place, src, ang, *shares, rot, go, radial, wig_back)
 
 
@@ -427,14 +461,12 @@
     quarter = (x_here + 2 * y_hi) % 4
     place = jnp.stack([core, quarter, 2 * quarter + core, edge_count.reshape(())])
 
-    sent = pack_own(place, so2_zero, so2_one, so2_two, feat_in)
+    sent, pair = pack_own(place, so2_zero, so2_one, so2_two, feat_in, ffn_in, grad_out)
+    pair_other = swap(pair, "core")
     got = lax.all_to_all(sent, ("z", "ylo"), 0, 0, tiled=True)
-    target_grad = ffn_backward(ffn_in, grad_out, ffn_up, ffn_down)
-    grads = target_grad[None]
-    for axis, mask in (("yhi", 2), ("yhi", 1), ("x", 2), ("x", 1), ("core", 1)):
-        count = 2 if axis == "core" else 4
-        other = lax.ppermute(grads, axis, [(at, at ^ mask) for at in range(count)])
-        grads = jnp.concatenate([grads, other], axis=0)
+    spread = ffn_backward(pair, pair_other, ffn_up, ffn_down)
+    grads = lax.all_to_all(spread, ("yhi", "x"), 0, 0, tiled=True)
+    grads = grads.reshape(32, PAD, C)
     got_other = swap(got, "core")
     own, half, feat = join_shares(place, got, got_other)
     turn = [(2 * at, 2 * ((at + 1) % 4)) for at in range(4)]
@@ -448,10 +480,7 @@
     src_slots = edge_src.reshape(-1)
     tgt_slots = edge_tgt.reshape(-1)
     angle_slots = edge_angle.reshape(-1)
-    y_turn = (tgt_slots // 8) ^ y_hi
-    x_turn = (tgt_slots // 2 % 4) ^ x_here
-    core_turn = (tgt_slots % 2) ^ core
-    tgt_piece = core_turn * 16 + x_turn % 2 * 8 + x_turn // 2 * 4 + y_turn % 2 * 2 + y_turn // 2
+    tgt_piece = tgt_slots // 2 * 2 + ((tgt_slots % 2) ^ core)
     wig = jnp.pad(wigner, ((0, 0), (0, 32 - KEEP), (0, PAD - COEF)))
     wig_back = jnp.transpose(wig, (0, 2, 1))
     rot, go = rotate_slots(src_slots, tgt_piece, angle_slots, feat, grads, wig)
@@ -459,7 +488,7 @@
         place, src_slots, angle_slots, shares, rot, go, edge_radial.reshape(128, C), wig_back
     )
     parts = lax.all_to_all(partial_sum, ("z", "ylo"), 0, 0, tiled=True)
-    total = target_grad.astype(F32) + jnp.sum(parts.astype(F32), axis=0)
+    total = spread[0, 0].astype(F32) + jnp.sum(parts.astype(F32), axis=0)
     return total[None, :COEF].astype(BF)
 
 

time: 157 us -> 142 us (0.904)
  the two profiles are of different devices: /device:TPU:6 before, /device:TPU:8 now
where the time goes in v1:
time: 142 us; the launch traced here: 141 us
  waiting for transfers between devices  40.2 us (28%)
  blocking collectives  38.8 us (27%)
  starting transfers between devices  29.7 us (21%)
  Pallas kernels  18.8 us (13%)
  local copies, waits for them, and re-layouts  11.6 us (8%)
    all_to_all x1, blocking collectives, body(): got = lax.all_to_all(sent, ('z', 'ylo'), 0, 0, tiled=True)  38.8 us
    ppermute x1, waiting for transfers between devices, body(): near = lax.ppermute(own, ('x', 'core'), turn)  15.8 us
    all_to_all x1, waiting for transfers between devices, body(): grads = lax.all_to_all(spread, ('yhi', 'x'), 0, 0, tiled=True)  10.6 us
    unnamed x43, local copies, waits for them, and re-layouts  10.2 us
    all_to_all x1, waiting for transfers between devices, body(): parts = lax.all_to_all(partial_sum, ('z', 'ylo'), 0, 0, tiled=True)  9.98 us
    pallas_call x1, Pallas kernels, edge_backward(): pl.pallas_call(edge_kernel, out_shape=jax.ShapeDtypeStruct((16, PAD, C),...  9 us
    ppermute x4, starting transfers between devices, swap(): return lax.ppermute(value, axis, [(0, 1), (1, 0)])  8.28 us
    all_to_all x1, starting transfers between devices, body(): grads = lax.all_to_all(spread, ('yhi', 'x'), 0, 0, tiled=True)  7.55 us
  transfers between devices with their start and end apart: 8, of which 5 were waited for; matrix products, arithmetic and copies ran while one was open for 3% of the time, Pallas kernels for 6%

profile of v1, /device:TPU:8, one launch (start us, length us, event | category | flops | bytes accessed | tf_op | source)
XLA Modules:
  0.0 140.7 jit_solution(12243366229244821661)
XLA Ops:
  0.7 0.9 copy-done.2
  1.6 0.9 copy-done.5
  2.5 0.9 copy-done.6
  3.4 0.7 copy-done.11
  4.2 0.7 copy-done.12
  4.9 0.7 copy-done.13
  5.6 0.7 shard_map.163
  6.4 38.8 %all_to_all.15.own_ref = bf16[16,248,128]{2,1,0:T(8,128)(2,1)S(1)} all-to-all(bf16[16,248,128]{2,1,0:T(8,128)(2,1)S(1)} %get-tuple-element.13), channel_id=1, replica_groups=mesh['yhi'=4,'x'=4,'core'=2,'z'=8,'ylo'=2] {'z','ylo'}, dimensions={0} | all-to-all | bytes 2031616 | tf_op jit(solution)/shard_map/all_to_all | solution.py:466
  45.2 2.0 %collective-permute-start.1 = (bf16[16,248,128]{2,1,0:T(8,128)(2,1)S(1)}, bf16[16,248,128]{2,1,0:T(8,128)(2,1)S(1)}, u32[]{:S(2)}, u32[]{:S(2)}) collective-permute-start(bf16[16,248,128]{2,1,0:T(8,128)(2,1)S(1)} %all_to_all.15.own_ref), channel_id=1, source_target_pairs={{0,16},{16,0},{1,17},{17,1},{2,18},{18,2},{3,19},{19,3},{4,20},{20... | collective-permute-start | bytes 3047432 | tf_op jit(solution)/shard_map/ppermute | solution.py:451
  47.3 2.6 %collective-permute-done.1.other_ref = bf16[16,248,128]{2,1,0:T(8,128)(2,1)S(1)} collective-permute-done((bf16[16,248,128]{2,1,0:T(8,128)(2,1)S(1)}, bf16[16,248,128]{2,1,0:T(8,128)(2,1)S(1)}, u32[]{:S(2)}, u32[]{:S(2)}) %collective-permute-start.1) | collective-permute-done | bytes 1015840 | tf_op jit(solution)/shard_map/ppermute | solution.py:451
  49.8 1.1 shard_map.165
  50.9 0.7 copy-done
  51.6 3.4 %collective-permute-start.2 = (bf16[2,3072,128]{2,1,0:T(8,128)(2,1)S(1)}, bf16[2,3072,128]{2,1,0:T(8,128)(2,1)}, u32[]{:S(2)}, u32[]{:S(2)}) collective-permute-start(bf16[2,3072,128]{2,1,0:T(8,128)(2,1)S(1)} %get-tuple-element.14.own_ref), channel_id=1, source_target_pairs={{0,32},{32,64},{64,96},{96,0},{16,112},{48,16},{80,48},{112,80},{1... | collective-permute-start | bytes 4718600 | tf_op jit(solution)/shard_map/ppermute | solution.py:474
  55.0 4.5 %collective-permute-start.4 = (bf16[2,1536,128]{2,1,0:T(8,128)(2,1)S(1)}, bf16[2,1536,128]{2,1,0:T(8,128)(2,1)}, u32[]{:S(2)}, u32[]{:S(2)}) collective-permute-start(bf16[2,1536,128]{2,1,0:T(8,128)(2,1)S(1)} %get-tuple-element.15), channel_id=1, source_target_pairs={{0,128},{128,256},{256,384},{384,0},{16,400},{144,16},{272,144},{4... | collective-permute-start | bytes 2359304 | tf_op jit(solution)/shard_map/ppermute | solution.py:475
  59.5 15.8 %collective-permute-done.2.near_ref = bf16[2,3072,128]{2,1,0:T(8,128)(2,1)} collective-permute-done((bf16[2,3072,128]{2,1,0:T(8,128)(2,1)S(1)}, bf16[2,3072,128]{2,1,0:T(8,128)(2,1)}, u32[]{:S(2)}, u32[]{:S(2)}) %collective-permute-start.2) | collective-permute-done | bytes 1572896 | tf_op jit(solution)/shard_map/ppermute | solution.py:474
  75.2 1.9 %collective-permute-start.3 = (bf16[2,3072,128]{2,1,0:T(8,128)(2,1)}, bf16[2,3072,128]{2,1,0:T(8,128)(2,1)}, u32[]{:S(2)}, u32[]{:S(2)}) collective-permute-start(bf16[2,3072,128]{2,1,0:T(8,128)(2,1)} %collective-permute-done.2.near_ref), channel_id=1, source_target_pairs={{0,16},{16,0},{1,17},{17,1},{2,18},{18,2},{3,19},{19,3},{4,20},{20... | collective-permute-start | bytes 4718600 | tf_op jit(solution)/shard_map/ppermute | solution.py:451
  77.2 2.4 %collective-permute-start = (bf16[2,56,128]{2,1,0:T(8,128)(2,1)S(1)}, bf16[2,56,128]{2,1,0:T(8,128)(2,1)S(1)}, u32[]{:S(2)}, u32[]{:S(2)}) collective-permute-start(bf16[2,56,128]{2,1,0:T(8,128)(2,1)S(1)} %get-tuple-element.12.own_ref), channel_id=1, source_target_pairs={{0,16},{16,0},{1,17},{17,1},{2,18},{18,2},{3,19},{19,3},{4,20},{20... | collective-permute-start | bytes 86024 | tf_op jit(solution)/shard_map/ppermute | solution.py:451
  79.6 1.3 collective-permute-done.other_ref
  80.9 2.1 %shard_map.164 = bf16[16,2,56,128]{3,2,1,0:T(8,128)(2,1)} custom-call(bf16[2,56,128]{2,1,0:T(8,128)(2,1)S(1)} %get-tuple-element.12.own_ref, bf16[2,56,128]{2,1,0:T(8,128)(2,1)S(1)} %collective-permute-done.other_ref, bf16[128,512]{1,0:T(8,128)(2,1)S(1)} %copy-done.3, bf16[512,128]{1,0:T(8,128)(2,1)S(1)} %copy-done.4, bf16[208,56]{1,0:T(8,128)(2,1)S(1)} %copy-done.8, ...), custom_call_target="tpu_custom_call" | custom-call | tf_op jit(solution)/shard_map/pallas_call | solution.py:217
  83.0 7.6 %all-to-all-start.1 = ((bf16[16,2,56,128]{3,2,1,0:T(8,128)(2,1)}), bf16[16,2,56,128]{3,2,1,0:T(8,128)(2,1)S(1)}, u32[]{:S(2)}, u32[]{:S(2)}) async-start(bf16[16,2,56,128]{3,2,1,0:T(8,128)(2,1)} %shard_map.164), calls=%async_computation.1 | async-start | bytes 917504 | tf_op jit(solution)/shard_map/all_to_all | solution.py:468
  90.6 1.9 %collective-permute-start.5 = (bf16[2,1536,128]{2,1,0:T(8,128)(2,1)}, bf16[2,1536,128]{2,1,0:T(8,128)(2,1)}, u32[]{:S(2)}, u32[]{:S(2)}) collective-permute-start(bf16[2,1536,128]{2,1,0:T(8,128)(2,1)} %collective-permute-done.4.half_ref), channel_id=1, source_target_pairs={{0,16},{16,0},{1,17},{17,1},{2,18},{18,2},{3,19},{19,3},{4,20},{20... | collective-permute-start | bytes 2359304 | tf_op jit(solution)/shard_map/ppermute | solution.py:451
  93.1 0.9 copy-done.16
  94.0 1.3 copy.20
  95.4 1.2 pad.4.clone.wig_ref
  96.9 10.6 %all-to-all-done.1 = bf16[16,2,56,128]{3,2,1,0:T(8,128)(2,1)S(1)} async-done(((bf16[16,2,56,128]{3,2,1,0:T(8,128)(2,1)}), bf16[16,2,56,128]{3,2,1,0:T(8,128)(2,1)S(1)}, u32[]{:S(2)}, u32[]{:S(2)}) %all-to-all-start.1) | async-done | bytes 458784 | tf_op jit(solution)/shard_map/all_to_all | solution.py:468
  107.5 0.9 copy-done.1
  108.5 5.9 %shard_map.166 = (bf16[4096,128]{1,0:T(8,128)(2,1)S(1)}, f32[4096,128]{1,0:T(8,128)S(1)}) custom-call(s32[128]{0:T(128)S(1)} %bitcast.31, s32[128]{0:T(128)S(1)} %fusion.3.tgt, s32[128]{0:T(128)S(1)} %bitcast.33, bf16[16,56,128]{2,1,0:T(8,128)(2,1)S(1)} %copy-done.1, bf16[32,56,128]{2,1,0:T(8,128)(2,1)S(1)} %bitcast.29, bf16[64,32,56]{2,1,0:T(8,128)(2,1)S(1)} %pad.4.clone.wig_ref), custom_call_target="tpu_custom_call" | custom-call | tf_op jit(solution)/shard_map/pallas_call | solution.py:245
  114.4 9.0 %shard_map.167 = bf16[16,56,128]{2,1,0:T(8,128)(2,1)} custom-call(s32[4]{0:T(128)S(1)} %pad_add_fusion.place, s32[128]{0:T(128)S(1)} %bitcast.32, s32[128]{0:T(128)S(1)} %bitcast.34, bf16[2,3072,128]{2,1,0:T(8,128)(2,1)S(1)} %get-tuple-element.14.own_ref, bf16[2,3072,128]{2,1,0:T(8,128)(2,1)} %collective-permute-done.2.near_ref, ...), custom_call_target="tpu_custom_call" | custom-call | tf_op jit(solution)/shard_map/pallas_call | solution.py:432
  123.4 6.0 %all-to-all-start.2 = ((bf16[16,56,128]{2,1,0:T(8,128)(2,1)}), bf16[16,56,128]{2,1,0:T(8,128)(2,1)S(1)}, u32[]{:S(2)}, u32[]{:S(2)}) async-start(bf16[16,56,128]{2,1,0:T(8,128)(2,1)} %shard_map.167), calls=%async_computation.2 | async-start | bytes 458752 | tf_op jit(solution)/shard_map/all_to_all | solution.py:490
  129.4 0.7 slice_bitcast_fusion
  130.1 10.0 %all-to-all-done.2 = bf16[16,56,128]{2,1,0:T(8,128)(2,1)S(1)} async-done(((bf16[16,56,128]{2,1,0:T(8,128)(2,1)}), bf16[16,56,128]{2,1,0:T(8,128)(2,1)S(1)}, u32[]{:S(2)}, u32[]{:S(2)}) %all-to-all-start.2) | async-done | bytes 229408 | tf_op jit(solution)/shard_map/all_to_all | solution.py:490
  140.1 0.6 fusion.1
  (39 shorter events, 1.0 us)
Async XLA Ops:
  0.7 0.9 copy-start.2
  1.6 0.9 copy-start.5
  2.5 0.9 copy-start.6
  3.4 0.7 copy-start.11
  4.1 0.7 copy-start.12
  4.9 0.7 copy-start.13
  6.3 74.6 %copy-start.3 = (bf16[128,512]{1,0:T(8,128)(2,1)S(1)}, bf16[128,512]{1,0:T(8,128)(2,1)}, u32[]{:S(2)}) copy-start(bf16[128,512]{1,0:T(8,128)(2,1)} %up_ref.1) | copy-start | bytes 393220
  6.3 74.6 %copy-start.4 = (bf16[512,128]{1,0:T(8,128)(2,1)S(1)}, bf16[512,128]{1,0:T(8,128)(2,1)}, u32[]{:S(2)}) copy-start(bf16[512,128]{1,0:T(8,128)(2,1)} %down_ref.1) | copy-start | bytes 393220
  6.3 74.5 %copy-start.7 = (bf16[208,56]{1,0:T(8,128)(2,1)S(1)}, bf16[208,56]{1,0:T(8,128)(2,1)}, u32[]{:S(2)}) copy-start(bf16[208,56]{1,0:T(8,128)(2,1)} %constant.82.from_ref) | copy-start | bytes 69892
  6.4 74.5 %copy-start.8 = (bf16[208,56]{1,0:T(8,128)(2,1)S(1)}, bf16[208,56]{1,0:T(8,128)(2,1)}, u32[]{:S(2)}) copy-start(bf16[208,56]{1,0:T(8,128)(2,1)} %constant.81.to_ref) | copy-start | bytes 69892
  6.4 74.5 %copy-start.10 = (bf16[56,208]{1,0:T(8,128)(2,1)S(1)}, bf16[56,208]{1,0:T(8,128)(2,1)}, u32[]{:S(2)}) copy-start(bf16[56,208]{1,0:T(8,128)(2,1)} %constant.83.back_ref) | copy-start | bytes 69892
  45.2 47.3 %copy-start.18 = (bf16[64,29,49]{0,1,2:T(8,128)(2,1)S(1)}, bf16[64,29,49]{0,1,2:T(8,128)(2,1)}, u32[]{:S(2)}) copy-start(bf16[64,29,49]{0,1,2:T(8,128)(2,1)} %param.25) | copy-start | bytes 545668
  45.2 4.6 %collective-permute-start.1 = (bf16[16,248,128]{2,1,0:T(8,128)(2,1)S(1)}, bf16[16,248,128]{2,1,0:T(8,128)(2,1)S(1)}, u32[]{:S(2)}, u32[]{:S(2)}) collective-permute-start(bf16[16,248,128]{2,1,0:T(8,128)(2,1)S(1)} %all_to_all.15.own_ref), channel_id=1, source_target_pairs={{0,16},{16,0},{1,17},{17,1},{2,18},{18,2},{3,19},{19,3},{4,20},{20... | collective-permute-start | bytes 3047432 | tf_op jit(solution)/shard_map/ppermute | solution.py:451
  50.9 0.7 copy-start
  51.6 23.6 %collective-permute-start.2 = (bf16[2,3072,128]{2,1,0:T(8,128)(2,1)S(1)}, bf16[2,3072,128]{2,1,0:T(8,128)(2,1)}, u32[]{:S(2)}, u32[]{:S(2)}) collective-permute-start(bf16[2,3072,128]{2,1,0:T(8,128)(2,1)S(1)} %get-tuple-element.14.own_ref), channel_id=1, source_target_pairs={{0,32},{32,64},{64,96},{96,0},{16,112},{48,16},{80,48},{112,80},{1... | collective-permute-start | bytes 4718600 | tf_op jit(solution)/shard_map/ppermute | solution.py:474
  55.0 35.5 %collective-permute-start.4 = (bf16[2,1536,128]{2,1,0:T(8,128)(2,1)S(1)}, bf16[2,1536,128]{2,1,0:T(8,128)(2,1)}, u32[]{:S(2)}, u32[]{:S(2)}) collective-permute-start(bf16[2,1536,128]{2,1,0:T(8,128)(2,1)S(1)} %get-tuple-element.15), channel_id=1, source_target_pairs={{0,128},{128,256},{256,384},{384,0},{16,400},{144,16},{272,144},{4... | collective-permute-start | bytes 2359304 | tf_op jit(solution)/shard_map/ppermute | solution.py:475
  75.2 39.1 %collective-permute-start.3 = (bf16[2,3072,128]{2,1,0:T(8,128)(2,1)}, bf16[2,3072,128]{2,1,0:T(8,128)(2,1)}, u32[]{:S(2)}, u32[]{:S(2)}) collective-permute-start(bf16[2,3072,128]{2,1,0:T(8,128)(2,1)} %collective-permute-done.2.near_ref), channel_id=1, source_target_pairs={{0,16},{16,0},{1,17},{17,1},{2,18},{18,2},{3,19},{19,3},{4,20},{20... | collective-permute-start | bytes 4718600 | tf_op jit(solution)/shard_map/ppermute | solution.py:451
  77.2 3.7 %collective-permute-start = (bf16[2,56,128]{2,1,0:T(8,128)(2,1)S(1)}, bf16[2,56,128]{2,1,0:T(8,128)(2,1)S(1)}, u32[]{:S(2)}, u32[]{:S(2)}) collective-permute-start(bf16[2,56,128]{2,1,0:T(8,128)(2,1)S(1)} %get-tuple-element.12.own_ref), channel_id=1, source_target_pairs={{0,16},{16,0},{1,17},{17,1},{2,18},{18,2},{3,19},{19,3},{4,20},{20... | collective-permute-start | bytes 86024 | tf_op jit(solution)/shard_map/ppermute | solution.py:451
  83.0 24.5 %all-to-all-start.1 = ((bf16[16,2,56,128]{3,2,1,0:T(8,128)(2,1)}), bf16[16,2,56,128]{3,2,1,0:T(8,128)(2,1)S(1)}, u32[]{:S(2)}, u32[]{:S(2)}) async-start(bf16[16,2,56,128]{3,2,1,0:T(8,128)(2,1)} %shard_map.164), calls=%async_computation.1 | async-start | bytes 917504 | tf_op jit(solution)/shard_map/all_to_all | solution.py:468
  90.6 23.8 %collective-permute-start.5 = (bf16[2,1536,128]{2,1,0:T(8,128)(2,1)}, bf16[2,1536,128]{2,1,0:T(8,128)(2,1)}, u32[]{:S(2)}, u32[]{:S(2)}) collective-permute-start(bf16[2,1536,128]{2,1,0:T(8,128)(2,1)} %collective-permute-done.4.half_ref), channel_id=1, source_target_pairs={{0,16},{16,0},{1,17},{17,1},{2,18},{18,2},{3,19},{19,3},{4,20},{20... | collective-permute-start | bytes 2359304 | tf_op jit(solution)/shard_map/ppermute | solution.py:451
  93.1 0.9 copy-start.16
  95.4 1.3 copy-start.17
  95.4 1.5 %copy-start.19 = (s32[1,1,128]{2,1,0:T(1,128)S(1)}, s32[1,1,128]{2,1,0:T(1,128)}, u32[]{:S(2)}) copy-start(s32[1,1,128]{2,1,0:T(1,128)} %param.27) | copy-start | bytes 1540
  95.4 12.2 %copy-start.14 = (s32[1,1,128]{2,1,0:T(1,128)S(1)}, s32[1,1,128]{2,1,0:T(1,128)}, u32[]{:S(2)}) copy-start(s32[1,1,128]{2,1,0:T(1,128)} %param.26) | copy-start | bytes 1540
  95.4 12.2 %copy-start.15 = (s32[1,1,128]{2,1,0:T(1,128)S(1)}, s32[1,1,128]{2,1,0:T(1,128)}, u32[]{:S(2)}) copy-start(s32[1,1,128]{2,1,0:T(1,128)} %param.28) | copy-start | bytes 1540
  96.7 17.6 %copy-start.9 = (bf16[1,1,128,128]{3,2,1,0:T(8,128)(2,1)S(1)}, bf16[1,1,128,128]{3,2,1,0:T(8,128)(2,1)}, u32[]{:S(2)}) copy-start(bf16[1,1,128,128]{3,2,1,0:T(8,128)(2,1)} %param.29) | copy-start | bytes 98308
  107.5 0.9 copy-start.1
  123.4 16.7 %all-to-all-start.2 = ((bf16[16,56,128]{2,1,0:T(8,128)(2,1)}), bf16[16,56,128]{2,1,0:T(8,128)(2,1)S(1)}, u32[]{:S(2)}, u32[]{:S(2)}) async-start(bf16[16,56,128]{2,1,0:T(8,128)(2,1)} %shard_map.167), calls=%async_computation.2 | async-start | bytes 458752 | tf_op jit(solution)/shard_map/all_to_all | solution.py:490

commit v2 on v0

--- a/solution.py
+++ b/solution.py
@@ -67,6 +67,10 @@
     return to_grid.astype(np.float32), from_grid.astype(np.float32)
 
 
+def grant(mebibytes):
+    return pltpu.CompilerParams(vmem_limit_bytes=mebibytes * 1024 * 1024)
+
+
 def dot(left, right):
     return jnp.dot(left, right, preferred_element_type=F32)
 
@@ -75,7 +79,11 @@
     return lax.dot_general(left, right, (((1,), (1,)), ((), ())), preferred_element_type=F32)
 
 
-def pack_kernel(place, zero_ref, one_ref, two_ref, feat_ref, out_ref):
+def pack_kernel(place, zero_ref, one_ref, two_ref, feat_ref, x_ref, g_ref, out_ref, pair_ref):
+    for row, ref in ((0, x_ref), (1, g_ref)):
+        pair_ref[row, 0:COEF, :] = ref[0]
+        pair_ref[row, COEF:PAD, :] = jnp.zeros((PAD - COEF, C), BF)
+
     for share in range(8):
 
         @pl.when(place[2] == share)
@@ -99,13 +107,17 @@
         out_ref[peer] = out_ref[0]
 
 
-def pack_own(place, so2_zero, so2_one, so2_two, feat_in):
+def pack_own(place, so2_zero, so2_one, so2_two, feat_in, ffn_in, grad_out):
+    vmem = pl.BlockSpec(memory_space=VMEM)
     return pl.pallas_call(
         pack_kernel,
-        out_shape=jax.ShapeDtypeStruct((16, SENT, C), BF),
-        in_specs=[pl.BlockSpec(memory_space=pltpu.SMEM)] + [pl.BlockSpec(memory_space=VMEM)] * 4,
-        out_specs=pl.BlockSpec(memory_space=VMEM),
-    )(place, so2_zero, so2_one, so2_two, feat_in)
+        out_shape=(
+            jax.ShapeDtypeStruct((16, SENT, C), BF),
+            jax.ShapeDtypeStruct((2, PAD, C), BF),
+        ),
+        in_specs=[pl.BlockSpec(memory_space=pltpu.SMEM)] + [vmem] * 6,
+        out_specs=(vmem, vmem),
+    )(place, so2_zero, so2_one, so2_two, feat_in, ffn_in, grad_out)
 
 
 def join_kernel(place, own_ref, other_ref, whole_ref, half_ref, feat_ref):
@@ -174,25 +186,23 @@
         ),
         in_specs=[pl.BlockSpec(memory_space=pltpu.SMEM), vmem, vmem],
         out_specs=(vmem,) * 3,
+        compiler_params=grant(16),
     )(place, own, other)
 
 
-def ffn_kernel(x_ref, g_ref, up_ref, down_ref, to_ref, from_ref, back_ref, out_ref, xs, gs):
-    xs[0:COEF, :] = x_ref[0]
-    xs[COEF:PAD, :] = jnp.zeros((PAD - COEF, C), BF)
-    gs[0:COEF, :] = g_ref[0]
-    gs[COEF:PAD, :] = jnp.zeros((PAD - COEF, C), BF)
-    grid_feat = dot(to_ref[...], xs[...]).astype(BF)
-    grad_value = dot(from_ref[...], gs[...]).astype(BF)
-    pre_act = dot(grid_feat, up_ref[...])
-    grad_act = dot_nt(grad_value, down_ref[...])
-    gate = jax.nn.sigmoid(pre_act)
-    grad_pre = (grad_act * gate * (1.0 + pre_act * (1.0 - gate))).astype(BF)
-    grad_grid = dot_nt(grad_pre, up_ref[...]).astype(BF)
-    out_ref[...] = (gs[...].astype(F32) + dot(back_ref[...], grad_grid)).astype(BF)
-
-
-def ffn_backward(ffn_in, grad_out, ffn_up, ffn_down):
+def ffn_kernel(own_ref, other_ref, up_ref, down_ref, to_ref, from_ref, back_ref, out_ref):
+    for place, ref in ((0, own_ref), (1, other_ref)):
+        grid_feat = dot(to_ref[...], ref[0]).astype(BF)
+        grad_value = dot(from_ref[...], ref[1]).astype(BF)
+        pre_act = dot(grid_feat, up_ref[...])
+        grad_act = dot_nt(grad_value, down_ref[...])
+        gate = jax.nn.sigmoid(pre_act)
+        grad_pre = (grad_act * gate * (1.0 + pre_act * (1.0 - gate))).astype(BF)
+        grad_grid = dot_nt(grad_pre, up_ref[...]).astype(BF)
+        out_ref[place] = (ref[1].astype(F32) + dot(back_ref[...], grad_grid)).astype(BF)
+
+
+def ffn_backward(own, other, ffn_up, ffn_down):
     to_grid, from_grid = sphere_tables(LMAX, GRID_SIDE)
     points = to_grid.shape[0]
     to_pad = np.zeros((208, PAD), np.float32)
@@ -203,15 +213,19 @@
     tables = [jnp.asarray(table, F32).astype(BF) for table in (to_pad, from_pad, back_pad)]
     return pl.pallas_call(
         ffn_kernel,
-        out_shape=jax.ShapeDtypeStruct((PAD, C), BF),
+        out_shape=jax.ShapeDtypeStruct((2, PAD, C), BF),
         in_specs=[pl.BlockSpec(memory_space=VMEM)] * 7,
         out_specs=pl.BlockSpec(memory_space=VMEM),
-        scratch_shapes=[VMEM((PAD, C), BF), VMEM((PAD, C), BF)],
-    )(ffn_in, grad_out, ffn_up, ffn_down, *tables)
-
-
-def rotate_kernel(src, tgt, ang, feat_ref, grad_ref, wig_ref, rot_ref, go_ref, acc):
+        compiler_params=grant(16),
+    )(own, other, ffn_up, ffn_down, *tables)
+
+
+def rotate_kernel(
+    src, tgt, ang, feat_ref, y0_ref, y1_ref, y2_ref, y3_ref, wig_ref, rot_ref, go_ref, acc, grad_ref
+):
     slots = 128
+    for back, ref in enumerate((y0_ref, y1_ref, y2_ref, y3_ref)):
+        grad_ref[8 * back : 8 * back + 8] = ref[...]
 
     def body(step, carry):
         for lane in range(8):
@@ -235,10 +249,11 @@
             jax.ShapeDtypeStruct((32 * 128, C), BF),
             jax.ShapeDtypeStruct((32 * 128, C), F32),
         ),
-        in_specs=[smem] * 3 + [vmem] * 3,
+        in_specs=[smem] * 3 + [vmem] * 6,
         out_specs=(vmem, vmem),
-        scratch_shapes=[VMEM((32 * 128, C), F32)],
-    )(src, tgt, ang, feat, grads, wig)
+        scratch_shapes=[VMEM((32 * 128, C), F32), VMEM((32, PAD, C), BF)],
+        compiler_params=grant(16),
+    )(src, tgt, ang, feat, *grads, wig)
 
 
 def edge_kernel(
@@ -409,8 +424,12 @@
             VMEM((32 * 128, C), F32),
             VMEM((16, PAD, C), F32),
         ],
-        compiler_params=pltpu.CompilerParams(vmem_limit_bytes=48 * 1024 * 1024),
+        compiler_params=grant(28),
     )(place, src, ang, *shares, rot, go, radial, wig_back)
+
+
+def shift(value, axis, count, step):
+    return lax.ppermute(value, axis, [(at, (at + step) % count) for at in range(count)])
 
 
 def swap(value, axis):
@@ -427,14 +446,17 @@
     quarter = (x_here + 2 * y_hi) % 4
     place = jnp.stack([core, quarter, 2 * quarter + core, edge_count.reshape(())])
 
-    sent = pack_own(place, so2_zero, so2_one, so2_two, feat_in)
+    sent, pair = pack_own(place, so2_zero, so2_one, so2_two, feat_in, ffn_in, grad_out)
+    pair_other = swap(pair, "core")
     got = lax.all_to_all(sent, ("z", "ylo"), 0, 0, tiled=True)
-    target_grad = ffn_backward(ffn_in, grad_out, ffn_up, ffn_down)
-    grads = target_grad[None]
-    for axis, mask in (("yhi", 2), ("yhi", 1), ("x", 2), ("x", 1), ("core", 1)):
-        count = 2 if axis == "core" else 4
-        other = lax.ppermute(grads, axis, [(at, at ^ mask) for at in range(count)])
-        grads = jnp.concatenate([grads, other], axis=0)
+    target_grads = ffn_backward(pair, pair_other, ffn_up, ffn_down)
+    grads = target_grads
+    for axis in ("x", "yhi"):
+        blocks = [grads]
+        for step in (1, 2, 3):
+            blocks.append(shift(grads, axis, 4, step))
+        if axis == "x":
+            grads = jnp.concatenate(blocks, axis=0)
     got_other = swap(got, "core")
     own, half, feat = join_shares(place, got, got_other)
     turn = [(2 * at, 2 * ((at + 1) % 4)) for at in range(4)]
@@ -448,18 +470,17 @@
     src_slots = edge_src.reshape(-1)
     tgt_slots = edge_tgt.reshape(-1)
     angle_slots = edge_angle.reshape(-1)
-    y_turn = (tgt_slots // 8) ^ y_hi
-    x_turn = (tgt_slots // 2 % 4) ^ x_here
-    core_turn = (tgt_slots % 2) ^ core
-    tgt_piece = core_turn * 16 + x_turn % 2 * 8 + x_turn // 2 * 4 + y_turn % 2 * 2 + y_turn // 2
+    y_back = (y_hi - tgt_slots // 8) % 4
+    x_back = (x_here - tgt_slots // 2 % 4) % 4
+    tgt_piece = (y_back * 4 + x_back) * 2 + ((tgt_slots % 2) ^ core)
     wig = jnp.pad(wigner, ((0, 0), (0, 32 - KEEP), (0, PAD - COEF)))
     wig_back = jnp.transpose(wig, (0, 2, 1))
-    rot, go = rotate_slots(src_slots, tgt_piece, angle_slots, feat, grads, wig)
+    rot, go = rotate_slots(src_slots, tgt_piece, angle_slots, feat, blocks, wig)
     partial_sum = edge_backward(
         place, src_slots, angle_slots, shares, rot, go, edge_radial.reshape(128, C), wig_back
     )
     parts = lax.all_to_all(partial_sum, ("z", "ylo"), 0, 0, tiled=True)
-    total = target_grad.astype(F32) + jnp.sum(parts.astype(F32), axis=0)
+    total = target_grads[0].astype(F32) + jnp.sum(parts.astype(F32), axis=0)
     return total[None, :COEF].astype(BF)
 
 

time: 157 us -> 149 us (0.949)
  blocking collectives: 52.4 us -> 39.1 us
  starting transfers between devices: 31.3 us -> 44.4 us
  waiting for transfers between devices: 26.1 us -> 34.2 us
  Pallas kernels: 26.8 us -> 19.8 us
  local copies, waits for them, and re-layouts: 12.9 us -> 6.42 us
  other arithmetic: 3.22 us -> 1.35 us
    all_to_all x1 -> x0, blocking collectives: 13.4 us -> none  [body(): parts = lax.all_to_all(partial_sum, ('z', 'ylo'), 0, 0, tiled=True)]
    all_to_all x0 -> x1, waiting for transfers between devices: none -> 9.47 us  [body(): parts = lax.all_to_all(partial_sum, ('z', 'ylo'), 0, 0, tiled=True)]
    ppermute x5 -> x6, starting transfers between devices: 18.5 us -> 25.5 us  [shift(): lax.ppermute(value, axis, [(at, (at + step) % count) for at in range(coun...]
    all_to_all x0 -> x1, starting transfers between devices: none -> 3.53 us  [body(): parts = lax.all_to_all(partial_sum, ('z', 'ylo'), 0, 0, tiled=True)]
    pallas_call x1, Pallas kernels: 8.54 us -> 5.2 us  [rotate_slots(): pl.pallas_call(rotate_kernel, out_shape=(jax.ShapeDtypeStruct((32 * 128,...]
    unnamed x28 -> x27, local copies, waits for them, and re-layouts: 8.29 us -> 4.99 us
    ppermute x3 -> x4, starting transfers between devices: 5.92 us -> 8.46 us  [swap(): return lax.ppermute(value, axis, [(0, 1), (1, 0)])]
    pallas_call x1, Pallas kernels: 3.46 us -> 1.03 us  [join_shares(): pl.pallas_call(join_kernel, out_shape=(jax.ShapeDtypeStruct((2, WHOLE, C)...]
  transfers between devices with their start and end apart: 10 -> 13, of which waited for: 5 -> 6; matrix products, arithmetic and copies ran while one was open for 8% -> 4% of each run, Pallas kernels for 7% -> 4%
where the time goes in v2:
time: 149 us; the launch traced here: 146 us
  starting transfers between devices  44.4 us (30%)
  blocking collectives  39.1 us (26%)
  waiting for transfers between devices  34.2 us (23%)
  Pallas kernels  19.8 us (13%)
  local copies, waits for them, and re-layouts  6.42 us (4%)
    all_to_all x1, blocking collectives, body(): got = lax.all_to_all(sent, ('z', 'ylo'), 0, 0, tiled=True)  39.1 us
    ppermute x6, starting transfers between devices, shift(): lax.ppermute(value, axis, [(at, (at + step) % count) for at in range(coun...  25.5 us
    ppermute x1, waiting for transfers between devices, body(): near = lax.ppermute(own, ('x', 'core'), turn)  15.4 us
    pallas_call x1, Pallas kernels, edge_backward(): pl.pallas_call(edge_kernel, out_shape=jax.ShapeDtypeStruct((16, PAD, C),...  10 us
    all_to_all x1, waiting for transfers between devices, body(): parts = lax.all_to_all(partial_sum, ('z', 'ylo'), 0, 0, tiled=True)  9.47 us
    ppermute x4, starting transfers between devices, swap(): return lax.ppermute(value, axis, [(0, 1), (1, 0)])  8.46 us
    ppermute x6, waiting for transfers between devices, shift(): lax.ppermute(value, axis, [(at, (at + step) % count) for at in range(coun...  5.74 us
    pallas_call x1, Pallas kernels, rotate_slots(): pl.pallas_call(rotate_kernel, out_shape=(jax.ShapeDtypeStruct((32 * 128,...  5.2 us
  transfers between devices with their start and end apart: 13, of which 6 were waited for; matrix products, arithmetic and copies ran while one was open for 4% of the time, Pallas kernels for 4%

profile of v2, /device:TPU:6, one launch (start us, length us, event | category | flops | bytes accessed | tf_op | source)
XLA Modules:
  0.0 146.2 jit_solution(14833349116547652563)
XLA Ops:
  0.7 0.7 pad_add_fusion.place
  1.3 2.2 %shard_map.163 = (bf16[16,248,128]{2,1,0:T(8,128)(2,1)}, bf16[2,56,128]{2,1,0:T(8,128)(2,1)}) custom-call(s32[4]{0:T(128)} %pad_add_fusion.place, bf16[56,1024]{1,0:T(8,128)(2,1)} %zero_ref.1, bf16[2,48,768]{2,1,0:T(8,128)(2,1)} %one_ref.1, bf16[2,40,640]{2,1,0:T(8,128)(2,1)} %two_ref.1, bf16[1,49,128]{2,1,0:T(8,128)(2,1)} %feat_ref.1, ...), custom_call_target="tpu_custom_call" | custom-call | tf_op jit(solution)/shard_map/pallas_call | solution.py:112
  3.6 0.0 copy-start.2
  3.6 39.1 %all_to_all.10.own_ref = bf16[16,248,128]{2,1,0:T(8,128)(2,1)S(1)} all-to-all(bf16[16,248,128]{2,1,0:T(8,128)(2,1)} %get-tuple-element.13), channel_id=1, replica_groups=mesh['yhi'=4,'x'=4,'core'=2,'z'=8,'ylo'=2] {'z','ylo'}, dimensions={0} | all-to-all | bytes 2031616 | tf_op jit(solution)/shard_map/all_to_all | solution.py:451
  42.7 2.0 %collective-permute-start.1 = (bf16[16,248,128]{2,1,0:T(8,128)(2,1)S(1)}, bf16[16,248,128]{2,1,0:T(8,128)(2,1)S(1)}, u32[]{:S(2)}, u32[]{:S(2)}) collective-permute-start(bf16[16,248,128]{2,1,0:T(8,128)(2,1)S(1)} %all_to_all.10.own_ref), channel_id=1, source_target_pairs={{0,16},{16,0},{1,17},{17,1},{2,18},{18,2},{3,19},{19,3},{4,20},{20... | collective-permute-start | bytes 3047432 | tf_op jit(solution)/shard_map/ppermute | solution.py:436
  44.7 2.6 %collective-permute-done.1.other_ref = bf16[16,248,128]{2,1,0:T(8,128)(2,1)S(1)} collective-permute-done((bf16[16,248,128]{2,1,0:T(8,128)(2,1)S(1)}, bf16[16,248,128]{2,1,0:T(8,128)(2,1)S(1)}, u32[]{:S(2)}, u32[]{:S(2)}) %collective-permute-start.1) | collective-permute-done | bytes 1015840 | tf_op jit(solution)/shard_map/ppermute | solution.py:436
  47.3 1.0 shard_map.165
  48.3 2.4 %collective-permute-start.2 = (bf16[2,3072,128]{2,1,0:T(8,128)(2,1)S(1)}, bf16[2,3072,128]{2,1,0:T(8,128)(2,1)S(1)}, u32[]{:S(2)}, u32[]{:S(2)}) collective-permute-start(bf16[2,3072,128]{2,1,0:T(8,128)(2,1)S(1)} %get-tuple-element.14.own_ref), channel_id=1, source_target_pairs={{0,32},{32,64},{64,96},{96,0},{16,112},{48,16},{80,48},{112,80},{1... | collective-permute-start | bytes 4718600 | tf_op jit(solution)/shard_map/ppermute | solution.py:464
  50.8 4.5 %collective-permute-start.4 = (bf16[2,1536,128]{2,1,0:T(8,128)(2,1)S(1)}, bf16[2,1536,128]{2,1,0:T(8,128)(2,1)}, u32[]{:S(2)}, u32[]{:S(2)}) collective-permute-start(bf16[2,1536,128]{2,1,0:T(8,128)(2,1)S(1)} %get-tuple-element.15), channel_id=1, source_target_pairs={{0,128},{128,256},{256,384},{384,0},{16,400},{144,16},{272,144},{4... | collective-permute-start | bytes 2359304 | tf_op jit(solution)/shard_map/ppermute | solution.py:465
  55.3 15.4 %collective-permute-done.2.near_ref = bf16[2,3072,128]{2,1,0:T(8,128)(2,1)S(1)} collective-permute-done((bf16[2,3072,128]{2,1,0:T(8,128)(2,1)S(1)}, bf16[2,3072,128]{2,1,0:T(8,128)(2,1)S(1)}, u32[]{:S(2)}, u32[]{:S(2)}) %collective-permute-start.2) | collective-permute-done | bytes 1572896 | tf_op jit(solution)/shard_map/ppermute | solution.py:464
  70.7 2.1 %collective-permute-start.3 = (bf16[2,3072,128]{2,1,0:T(8,128)(2,1)S(1)}, bf16[2,3072,128]{2,1,0:T(8,128)(2,1)}, u32[]{:S(2)}, u32[]{:S(2)}) collective-permute-start(bf16[2,3072,128]{2,1,0:T(8,128)(2,1)S(1)} %collective-permute-done.2.near_ref), channel_id=1, source_target_pairs={{0,16},{16,0},{1,17},{17,1},{2,18},{18,2},{3,19},{19,3},{4,20},{20... | collective-permute-start | bytes 4718600 | tf_op jit(solution)/shard_map/ppermute | solution.py:436
  72.8 2.2 %collective-permute-start.5 = (bf16[2,1536,128]{2,1,0:T(8,128)(2,1)}, bf16[2,1536,128]{2,1,0:T(8,128)(2,1)}, u32[]{:S(2)}, u32[]{:S(2)}) collective-permute-start(bf16[2,1536,128]{2,1,0:T(8,128)(2,1)} %collective-permute-done.4.half_ref), channel_id=1, source_target_pairs={{0,16},{16,0},{1,17},{17,1},{2,18},{18,2},{3,19},{19,3},{4,20},{20... | collective-permute-start | bytes 2359304 | tf_op jit(solution)/shard_map/ppermute | solution.py:436
  75.0 2.1 %collective-permute-start = (bf16[2,56,128]{2,1,0:T(8,128)(2,1)S(1)}, bf16[2,56,128]{2,1,0:T(8,128)(2,1)S(1)}, u32[]{:S(2)}, u32[]{:S(2)}) collective-permute-start(bf16[2,56,128]{2,1,0:T(8,128)(2,1)S(1)} %copy-done.6), channel_id=1, source_target_pairs={{0,16},{16,0},{1,17},{17,1},{2,18},{18,2},{3,19},{19,3},{4,20},{20... | collective-permute-start | bytes 86024 | tf_op jit(solution)/shard_map/ppermute | solution.py:436
  77.1 1.0 collective-permute-done.other_ref
  78.1 1.3 shard_map.164
  79.4 3.6 %collective-permute-start.6 = (bf16[2,56,128]{2,1,0:T(8,128)(2,1)S(1)}, bf16[2,56,128]{2,1,0:T(8,128)(2,1)S(1)}, u32[]{:S(2)}, u32[]{:S(2)}) collective-permute-start(bf16[2,56,128]{2,1,0:T(8,128)(2,1)S(1)} %shard_map.164), channel_id=1, source_target_pairs={{0,32},{32,64},{64,96},{96,0},{1,33},{33,65},{65,97},{97,1},{2,34}... | collective-permute-start | bytes 86024 | tf_op jit(solution)/shard_map/ppermute | solution.py:432
  83.1 3.1 %collective-permute-start.7 = (bf16[2,56,128]{2,1,0:T(8,128)(2,1)S(1)}, bf16[2,56,128]{2,1,0:T(8,128)(2,1)S(1)}, u32[]{:S(2)}, u32[]{:S(2)}) collective-permute-start(bf16[2,56,128]{2,1,0:T(8,128)(2,1)S(1)} %shard_map.164), channel_id=1, source_target_pairs={{0,64},{32,96},{64,0},{96,32},{1,65},{33,97},{65,1},{97,33},{2,66}... | collective-permute-start | bytes 86024 | tf_op jit(solution)/shard_map/ppermute | solution.py:432
  86.2 1.9 %collective-permute-start.8 = (bf16[2,56,128]{2,1,0:T(8,128)(2,1)S(1)}, bf16[2,56,128]{2,1,0:T(8,128)(2,1)S(1)}, u32[]{:S(2)}, u32[]{:S(2)}) collective-permute-start(bf16[2,56,128]{2,1,0:T(8,128)(2,1)S(1)} %shard_map.164), channel_id=1, source_target_pairs={{0,96},{32,0},{64,32},{96,64},{1,97},{33,1},{65,33},{97,65},{2,98}... | collective-permute-start | bytes 86024 | tf_op jit(solution)/shard_map/ppermute | solution.py:432
  88.2 2.4 %copy.18 = bf16[64,29,49]{1,2,0:T(8,128)(2,1)} copy(bf16[64,29,49]{0,1,2:T(8,128)(2,1)} %param.25) | data formatting | bytes 363776 | tf_op args[8]
  90.6 2.5 %copy.20 = bf16[64,29,49]{2,1,0:T(8,128)(2,1)} copy(bf16[64,29,49]{1,2,0:T(8,128)(2,1)} %copy.18) | data formatting | bytes 363776
  93.1 1.2 pad.4.clone.wig_ref
  94.4 10.1 %collective-permute-start.10 = (bf16[8,56,128]{2,1,0:T(8,128)(2,1)S(1)}, bf16[8,56,128]{2,1,0:T(8,128)(2,1)S(1)}, u32[]{:S(2)}, u32[]{:S(2)}) collective-permute-start(bf16[8,56,128]{2,1,0:T(8,128)(2,1)S(1)} %pad_maximum_fusion.y0_ref), channel_id=1, source_target_pairs={{0,256},{128,384},{256,0},{384,128},{1,257},{129,385},{257,1},{385... | collective-permute-start | bytes 344072 | tf_op jit(solution)/shard_map/ppermute | solution.py:432
  104.5 1.9 %collective-permute-start.11 = (bf16[8,56,128]{2,1,0:T(8,128)(2,1)S(1)}, bf16[8,56,128]{2,1,0:T(8,128)(2,1)S(1)}, u32[]{:S(2)}, u32[]{:S(2)}) collective-permute-start(bf16[8,56,128]{2,1,0:T(8,128)(2,1)S(1)} %pad_maximum_fusion.y0_ref), channel_id=1, source_target_pairs={{0,384},{128,0},{256,128},{384,256},{1,385},{129,1},{257,129},{385... | collective-permute-start | bytes 344072 | tf_op jit(solution)/shard_map/ppermute | solution.py:432
  106.5 4.8 %collective-permute-start.9 = (bf16[8,56,128]{2,1,0:T(8,128)(2,1)S(1)}, bf16[8,56,128]{2,1,0:T(8,128)(2,1)S(1)}, u32[]{:S(2)}, u32[]{:S(2)}) collective-permute-start(bf16[8,56,128]{2,1,0:T(8,128)(2,1)S(1)} %pad_maximum_fusion.y0_ref), channel_id=1, source_target_pairs={{0,128},{128,256},{256,384},{384,0},{1,129},{129,257},{257,385},{3... | collective-permute-start | bytes 344072 | tf_op jit(solution)/shard_map/ppermute | solution.py:432
  111.3 0.2 pad_bitcast_fusion.wig_ref
  111.5 3.9 %collective-permute-done.11.y3_ref = bf16[8,56,128]{2,1,0:T(8,128)(2,1)S(1)} collective-permute-done((bf16[8,56,128]{2,1,0:T(8,128)(2,1)S(1)}, bf16[8,56,128]{2,1,0:T(8,128)(2,1)S(1)}, u32[]{:S(2)}, u32[]{:S(2)}) %collective-permute-start.11) | collective-permute-done | bytes 114720 | tf_op jit(solution)/shard_map/ppermute | solution.py:432
  115.4 1.8 %collective-permute-done.9.y1_ref = bf16[8,56,128]{2,1,0:T(8,128)(2,1)S(1)} collective-permute-done((bf16[8,56,128]{2,1,0:T(8,128)(2,1)S(1)}, bf16[8,56,128]{2,1,0:T(8,128)(2,1)S(1)}, u32[]{:S(2)}, u32[]{:S(2)}) %collective-permute-start.9) | collective-permute-done | bytes 114720 | tf_op jit(solution)/shard_map/ppermute | solution.py:432
  117.2 5.2 %shard_map.166 = (bf16[4096,128]{1,0:T(8,128)(2,1)S(1)}, f32[4096,128]{1,0:T(8,128)S(1)}) custom-call(s32[128]{0:T(128)S(1)} %bitcast.32, s32[128]{0:T(128)S(1)} %fusion.6.tgt, s32[128]{0:T(128)S(1)} %bitcast.34, bf16[16,56,128]{2,1,0:T(8,128)(2,1)S(1)} %get-tuple-element.16.feat_ref, bf16[8,56,128]{2,1,0:T(8,128)(2,1)S(1)} %pad_maximum_fusion.y0_ref, ...), custom_call_target="tpu_custom_call" | custom-call | tf_op jit(solution)/shard_map/pallas_call | solution.py:246
  122.5 10.0 %shard_map.167 = bf16[16,56,128]{2,1,0:T(8,128)(2,1)} custom-call(s32[4]{0:T(128)S(1)} %copy-done.7, s32[128]{0:T(128)S(1)} %bitcast.33, s32[128]{0:T(128)S(1)} %bitcast.35, bf16[2,3072,128]{2,1,0:T(8,128)(2,1)S(1)} %get-tuple-element.14.own_ref, bf16[2,3072,128]{2,1,0:T(8,128)(2,1)S(1)} %collective-permute-done.2.near_ref, ...), custom_call_target="tpu_custom_call" | custom-call | tf_op jit(solution)/shard_map/pallas_call | solution.py:414
  132.5 3.5 %all-to-all-start.1 = ((bf16[16,56,128]{2,1,0:T(8,128)(2,1)}), bf16[16,56,128]{2,1,0:T(8,128)(2,1)S(1)}, u32[]{:S(2)}, u32[]{:S(2)}) async-start(bf16[16,56,128]{2,1,0:T(8,128)(2,1)} %shard_map.167), calls=%async_computation.1 | async-start | bytes 458752 | tf_op jit(solution)/shard_map/all_to_all | solution.py:482
  136.1 9.5 %all-to-all-done.1 = bf16[16,56,128]{2,1,0:T(8,128)(2,1)S(1)} async-done(((bf16[16,56,128]{2,1,0:T(8,128)(2,1)}), bf16[16,56,128]{2,1,0:T(8,128)(2,1)S(1)}, u32[]{:S(2)}, u32[]{:S(2)}) %all-to-all-start.1) | async-done | bytes 229408 | tf_op jit(solution)/shard_map/all_to_all | solution.py:482
  145.6 0.6 fusion.1
  (34 shorter events, 0.2 us)
Async XLA Ops:
  1.3 46.0 %copy-start.7 = (s32[4]{0:T(128)S(1)}, s32[4]{0:T(128)}, u32[]{:S(2)}) copy-start(s32[4]{0:T(128)} %pad_add_fusion.place) | copy-start | bytes 52
  3.5 71.5 %copy-start.6 = (bf16[2,56,128]{2,1,0:T(8,128)(2,1)S(1)}, bf16[2,56,128]{2,1,0:T(8,128)(2,1)}, u32[]{:S(2)}) copy-start(bf16[2,56,128]{2,1,0:T(8,128)(2,1)} %get-tuple-element.12.own_ref) | copy-start | bytes 86020
  3.5 74.6 %copy-start = (bf16[128,512]{1,0:T(8,128)(2,1)S(1)}, bf16[128,512]{1,0:T(8,128)(2,1)}, u32[]{:S(2)}) copy-start(bf16[128,512]{1,0:T(8,128)(2,1)} %up_ref.1) | copy-start | bytes 393220
  3.5 74.6 %copy-start.1 = (bf16[512,128]{1,0:T(8,128)(2,1)S(1)}, bf16[512,128]{1,0:T(8,128)(2,1)}, u32[]{:S(2)}) copy-start(bf16[512,128]{1,0:T(8,128)(2,1)} %down_ref.1) | copy-start | bytes 393220
  3.6 74.6 %copy-start.2 = (bf16[208,56]{1,0:T(8,128)(2,1)S(1)}, bf16[208,56]{1,0:T(8,128)(2,1)}, u32[]{:S(2)}) copy-start(bf16[208,56]{1,0:T(8,128)(2,1)} %constant.107.to_ref) | copy-start | bytes 69892
  3.6 74.5 %copy-start.3 = (bf16[208,56]{1,0:T(8,128)(2,1)S(1)}, bf16[208,56]{1,0:T(8,128)(2,1)}, u32[]{:S(2)}) copy-start(bf16[208,56]{1,0:T(8,128)(2,1)} %constant.108.from_ref) | copy-start | bytes 69892
  3.6 74.5 %copy-start.5 = (bf16[56,208]{1,0:T(8,128)(2,1)S(1)}, bf16[56,208]{1,0:T(8,128)(2,1)}, u32[]{:S(2)}) copy-start(bf16[56,208]{1,0:T(8,128)(2,1)} %constant.109.back_ref) | copy-start | bytes 69892
  42.7 45.5 %copy-start.11 = (s32[1,1,128]{2,1,0:T(1,128)S(1)}, s32[1,1,128]{2,1,0:T(1,128)}, u32[]{:S(2)}) copy-start(s32[1,1,128]{2,1,0:T(1,128)} %param.27) | copy-start | bytes 1540
  42.7 4.6 %collective-permute-start.1 = (bf16[16,248,128]{2,1,0:T(8,128)(2,1)S(1)}, bf16[16,248,128]{2,1,0:T(8,128)(2,1)S(1)}, u32[]{:S(2)}, u32[]{:S(2)}) collective-permute-start(bf16[16,248,128]{2,1,0:T(8,128)(2,1)S(1)} %all_to_all.10.own_ref), channel_id=1, source_target_pairs={{0,16},{16,0},{1,17},{17,1},{2,18},{18,2},{3,19},{19,3},{4,20},{20... | collective-permute-start | bytes 3047432 | tf_op jit(solution)/shard_map/ppermute | solution.py:436
  48.3 22.3 %collective-permute-start.2 = (bf16[2,3072,128]{2,1,0:T(8,128)(2,1)S(1)}, bf16[2,3072,128]{2,1,0:T(8,128)(2,1)S(1)}, u32[]{:S(2)}, u32[]{:S(2)}) collective-permute-start(bf16[2,3072,128]{2,1,0:T(8,128)(2,1)S(1)} %get-tuple-element.14.own_ref), channel_id=1, source_target_pairs={{0,32},{32,64},{64,96},{96,0},{16,112},{48,16},{80,48},{112,80},{1... | collective-permute-start | bytes 4718600 | tf_op jit(solution)/shard_map/ppermute | solution.py:464
  50.8 22.0 %collective-permute-start.4 = (bf16[2,1536,128]{2,1,0:T(8,128)(2,1)S(1)}, bf16[2,1536,128]{2,1,0:T(8,128)(2,1)}, u32[]{:S(2)}, u32[]{:S(2)}) collective-permute-start(bf16[2,1536,128]{2,1,0:T(8,128)(2,1)S(1)} %get-tuple-element.15), channel_id=1, source_target_pairs={{0,128},{128,256},{256,384},{384,0},{16,400},{144,16},{272,144},{4... | collective-permute-start | bytes 2359304 | tf_op jit(solution)/shard_map/ppermute | solution.py:465
  70.7 51.8 %collective-permute-start.3 = (bf16[2,3072,128]{2,1,0:T(8,128)(2,1)S(1)}, bf16[2,3072,128]{2,1,0:T(8,128)(2,1)}, u32[]{:S(2)}, u32[]{:S(2)}) collective-permute-start(bf16[2,3072,128]{2,1,0:T(8,128)(2,1)S(1)} %collective-permute-done.2.near_ref), channel_id=1, source_target_pairs={{0,16},{16,0},{1,17},{17,1},{2,18},{18,2},{3,19},{19,3},{4,20},{20... | collective-permute-start | bytes 4718600 | tf_op jit(solution)/shard_map/ppermute | solution.py:436
  72.8 49.7 %collective-permute-start.5 = (bf16[2,1536,128]{2,1,0:T(8,128)(2,1)}, bf16[2,1536,128]{2,1,0:T(8,128)(2,1)}, u32[]{:S(2)}, u32[]{:S(2)}) collective-permute-start(bf16[2,1536,128]{2,1,0:T(8,128)(2,1)} %collective-permute-done.4.half_ref), channel_id=1, source_target_pairs={{0,16},{16,0},{1,17},{17,1},{2,18},{18,2},{3,19},{19,3},{4,20},{20... | collective-permute-start | bytes 2359304 | tf_op jit(solution)/shard_map/ppermute | solution.py:436
  75.0 3.1 %collective-permute-start = (bf16[2,56,128]{2,1,0:T(8,128)(2,1)S(1)}, bf16[2,56,128]{2,1,0:T(8,128)(2,1)S(1)}, u32[]{:S(2)}, u32[]{:S(2)}) collective-permute-start(bf16[2,56,128]{2,1,0:T(8,128)(2,1)S(1)} %copy-done.6), channel_id=1, source_target_pairs={{0,16},{16,0},{1,17},{17,1},{2,18},{18,2},{3,19},{19,3},{4,20},{20... | collective-permute-start | bytes 86024 | tf_op jit(solution)/shard_map/ppermute | solution.py:436
  79.4 14.9 %collective-permute-start.6 = (bf16[2,56,128]{2,1,0:T(8,128)(2,1)S(1)}, bf16[2,56,128]{2,1,0:T(8,128)(2,1)S(1)}, u32[]{:S(2)}, u32[]{:S(2)}) collective-permute-start(bf16[2,56,128]{2,1,0:T(8,128)(2,1)S(1)} %shard_map.164), channel_id=1, source_target_pairs={{0,32},{32,64},{64,96},{96,0},{1,33},{33,65},{65,97},{97,1},{2,34}... | collective-permute-start | bytes 86024 | tf_op jit(solution)/shard_map/ppermute | solution.py:432
  83.1 11.3 %collective-permute-start.7 = (bf16[2,56,128]{2,1,0:T(8,128)(2,1)S(1)}, bf16[2,56,128]{2,1,0:T(8,128)(2,1)S(1)}, u32[]{:S(2)}, u32[]{:S(2)}) collective-permute-start(bf16[2,56,128]{2,1,0:T(8,128)(2,1)S(1)} %shard_map.164), channel_id=1, source_target_pairs={{0,64},{32,96},{64,0},{96,32},{1,65},{33,97},{65,1},{97,33},{2,66}... | collective-permute-start | bytes 86024 | tf_op jit(solution)/shard_map/ppermute | solution.py:432
  86.2 8.2 %collective-permute-start.8 = (bf16[2,56,128]{2,1,0:T(8,128)(2,1)S(1)}, bf16[2,56,128]{2,1,0:T(8,128)(2,1)S(1)}, u32[]{:S(2)}, u32[]{:S(2)}) collective-permute-start(bf16[2,56,128]{2,1,0:T(8,128)(2,1)S(1)} %shard_map.164), channel_id=1, source_target_pairs={{0,96},{32,0},{64,32},{96,64},{1,97},{33,1},{65,33},{97,65},{2,98}... | collective-permute-start | bytes 86024 | tf_op jit(solution)/shard_map/ppermute | solution.py:432
  93.1 18.2 %copy-start.10 = (bf16[64,29,49]{1,2,0:T(8,128)(2,1)S(1)}, bf16[64,29,49]{1,2,0:T(8,128)(2,1)}, u32[]{:S(2)}) copy-start(bf16[64,29,49]{1,2,0:T(8,128)(2,1)} %copy.18) | copy-start | bytes 545668
  93.1 24.1 %copy-start.8 = (s32[1,1,128]{2,1,0:T(1,128)S(1)}, s32[1,1,128]{2,1,0:T(1,128)}, u32[]{:S(2)}) copy-start(s32[1,1,128]{2,1,0:T(1,128)} %param.26) | copy-start | bytes 1540
  93.1 24.1 %copy-start.9 = (s32[1,1,128]{2,1,0:T(1,128)S(1)}, s32[1,1,128]{2,1,0:T(1,128)}, u32[]{:S(2)}) copy-start(s32[1,1,128]{2,1,0:T(1,128)} %param.28) | copy-start | bytes 1540
  94.4 28.1 %copy-start.4 = (bf16[1,1,128,128]{3,2,1,0:T(8,128)(2,1)S(1)}, bf16[1,1,128,128]{3,2,1,0:T(8,128)(2,1)}, u32[]{:S(2)}) copy-start(bf16[1,1,128,128]{3,2,1,0:T(8,128)(2,1)} %param.29) | copy-start | bytes 98308
  94.4 17.1 %collective-permute-start.10 = (bf16[8,56,128]{2,1,0:T(8,128)(2,1)S(1)}, bf16[8,56,128]{2,1,0:T(8,128)(2,1)S(1)}, u32[]{:S(2)}, u32[]{:S(2)}) collective-permute-start(bf16[8,56,128]{2,1,0:T(8,128)(2,1)S(1)} %pad_maximum_fusion.y0_ref), channel_id=1, source_target_pairs={{0,256},{128,384},{256,0},{384,128},{1,257},{129,385},{257,1},{385... | collective-permute-start | bytes 344072 | tf_op jit(solution)/shard_map/ppermute | solution.py:432
  104.5 10.9 %collective-permute-start.11 = (bf16[8,56,128]{2,1,0:T(8,128)(2,1)S(1)}, bf16[8,56,128]{2,1,0:T(8,128)(2,1)S(1)}, u32[]{:S(2)}, u32[]{:S(2)}) collective-permute-start(bf16[8,56,128]{2,1,0:T(8,128)(2,1)S(1)} %pad_maximum_fusion.y0_ref), channel_id=1, source_target_pairs={{0,384},{128,0},{256,128},{384,256},{1,385},{129,1},{257,129},{385... | collective-permute-start | bytes 344072 | tf_op jit(solution)/shard_map/ppermute | solution.py:432
  106.5 10.8 %collective-permute-start.9 = (bf16[8,56,128]{2,1,0:T(8,128)(2,1)S(1)}, bf16[8,56,128]{2,1,0:T(8,128)(2,1)S(1)}, u32[]{:S(2)}, u32[]{:S(2)}) collective-permute-start(bf16[8,56,128]{2,1,0:T(8,128)(2,1)S(1)} %pad_maximum_fusion.y0_ref), channel_id=1, source_target_pairs={{0,128},{128,256},{256,384},{384,0},{1,129},{129,257},{257,385},{3... | collective-permute-start | bytes 344072 | tf_op jit(solution)/shard_map/ppermute | solution.py:432
  132.5 13.0 %all-to-all-start.1 = ((bf16[16,56,128]{2,1,0:T(8,128)(2,1)}), bf16[16,56,128]{2,1,0:T(8,128)(2,1)S(1)}, u32[]{:S(2)}, u32[]{:S(2)}) async-start(bf16[16,56,128]{2,1,0:T(8,128)(2,1)} %shard_map.167), calls=%async_computation.1 | async-start | bytes 458752 | tf_op jit(solution)/shard_map/all_to_all | solution.py:482
